TPU v7x, 1024 devices: a whole 4x8x16 slice. The times are simulated.
1024 devices in a mesh: grp: 4 (over z_hi, core), lat: 8 (over z_lo), lon: 32 (over y, x).
Axes of the slice: x: 4, y: 8, z: 16 (z_hi: 2, z_lo: 8; z = z_hi * 8 + z_lo), core: 2. Of those that a mesh axis runs over, the one named last changes fastest.
Arguments:
- state: float32 [5, 128, 256, 512], P(None, 'lon', 'lat', 'grp'), may hold values from -5 to 5
- tracers: float32 [12, 256, 512, 128], P(None, 'lat', ('grp', 'lon')), may hold values from 0.1 to 1.5
- coupling: float32 [5, 5], replicated, may hold values from -0.8 to 0.8
- rates: float32 [24], replicated, may hold values from 0.05 to 0.5
- pairs: int32 [24, 3], replicated, may hold values from 0 to 11
- heat_map: int32 [12], replicated, may hold values from 0 to 3
- heat_coef: float32 [4], replicated, may hold values from 0.5 to 2
Outputs:
- state_out: float32 [5, 128, 256, 512], P(None, 'lon', 'lat', 'grp')
- tracers_out: float32 [12, 256, 512, 128], P(None, 'lat', ('grp', 'lon'))
All inputs are finite; a program needn't handle non-finite values.
Results may differ from a plain program's by a relative error of at most 0.000052.
Values sent between devices are 32-bit elements; how exact they have to be, the bound alone decides.
No kernel may reach another device: no remote copies, remote signals or barrier semaphores. Data moves between devices by JAX's collectives and lax.ppermute only.
A program may use at most 32 MiB of HBM per device.

v0:
```python
import jax
import jax.numpy as jnp
from jax import lax
from jax.sharding import PartitionSpec as P

HIGH = lax.Precision.HIGHEST


def extended(block, sides, width, periodic):
    for axis, dim in sides:
        count = lax.axis_size(axis)
        forward = [(i, i + 1) for i in range(count - 1)]
        if periodic:
            forward.append((count - 1, 0))
        backward = [(target, source) for source, target in forward]
        low = lax.ppermute(
            lax.slice_in_dim(block, block.shape[dim] - width, None, axis=dim), axis, forward
        )
        high = lax.ppermute(lax.slice_in_dim(block, 0, width, axis=dim), axis, backward)
        block = jnp.concatenate([low, block, high], axis=dim)
    return block


def stencil(center, plus_one, plus_two, minus_one, minus_two):
    advect = -(8.0 * (plus_one - minus_one) - (plus_two - minus_two)) * (0.3 / 12.0)
    return advect + 0.1 * (plus_one + minus_one - 2.0 * center)


def tendency(fields, coupling):
    padded_x = extended(fields, (("lat", 2),), 2, False)
    padded_y = extended(fields, (("grp", 3),), 2, True)
    along_x = stencil(
        fields, padded_x[:, :, 3:-1], padded_x[:, :, 4:], padded_x[:, :, 1:-3], padded_x[:, :, :-4]
    )
    along_y = stencil(
        fields,
        padded_y[:, :, :, 3:-1],
        padded_y[:, :, :, 4:],
        padded_y[:, :, :, 1:-3],
        padded_y[:, :, :, :-4],
    )
    mixed = jnp.einsum("fg,gzxy->fzxy", coupling, fields, precision=HIGH)
    return along_x + along_y + mixed


def clamped(field, axis):
    length = field.shape[axis]
    higher = jnp.concatenate(
        [
            lax.slice_in_dim(field, 1, length, axis=axis),
            lax.slice_in_dim(field, length - 1, length, axis=axis),
        ],
        axis,
    )
    lower = jnp.concatenate(
        [
            lax.slice_in_dim(field, 0, 1, axis=axis),
            lax.slice_in_dim(field, 0, length - 1, axis=axis),
        ],
        axis,
    )
    return (higher, lower)


def mixing_of(east_diff, north_diff):
    shear = east_diff * east_diff + north_diff * north_diff
    return 0.2 * shear / (1.0 + shear)


def column_step(species, mixing_k, vertical, rates, pairs, heat_map, heat_coef):
    speed = 0.4 * vertical / (1.0 + jnp.abs(vertical))
    rising = jnp.maximum(speed, 0.0)
    sinking = jnp.minimum(speed, 0.0)
    higher, lower = clamped(species, 2)
    advect = -rising * (species - lower) - sinking * (higher - species)
    diffuse = mixing_k * (higher - 2.0 * species + lower)
    flat = species.reshape(species.shape[0], -1)
    labels = jnp.arange(species.shape[0], dtype=jnp.int32)
    first = (pairs[:, 0:1] == labels[None, :]).astype(jnp.float32)
    second = (pairs[:, 1:2] == labels[None, :]).astype(jnp.float32)
    product = (pairs[:, 2:3] == labels[None, :]).astype(jnp.float32)
    conc_a = jnp.dot(first, flat, precision=HIGH)
    conc_b = jnp.dot(second, flat, precision=HIGH)
    reaction = rates[:, None] * conc_a * conc_b
    stoich = product - first - second
    change = jnp.dot(stoich.T, reaction, precision=HIGH)
    classes = jnp.arange(heat_coef.shape[0], dtype=jnp.int32)
    weights = jnp.dot(
        (heat_map[:, None] == classes[None, :]).astype(jnp.float32), heat_coef, precision=HIGH
    )
    heat = jnp.dot(weights, change, precision=HIGH)
    renewed = species + advect + diffuse + change.reshape(species.shape)
    return (renewed, heat.reshape(mixing_k.shape))


def on_device(state, tracers, coupling, rates, pairs, heat_map, heat_coef):
    section_one = state + tendency(state, coupling)
    section_two = 0.75 * state + 0.25 * (section_one + tendency(section_one, coupling))
    stepped = state / 3.0 + 2.0 / 3.0 * (section_two + tendency(section_two, coupling))
    cols_x = tracers.shape[1]
    cols_y = tracers.shape[2]
    levels_all = tracers.shape[3]
    columns = cols_x * cols_y
    outgoing = jnp.transpose(stepped[0:3], (0, 2, 3, 1))
    regrouped = lax.all_to_all(outgoing, "lon", split_axis=2, concat_axis=3, tiled=True)
    regrouped = regrouped.reshape(3, columns, levels_all)
    higher, lower = clamped(regrouped[0:2], 2)
    diffs = higher - lower
    mixing_k = mixing_of(diffs[0], diffs[1])
    vertical = regrouped[2]
    species = tracers.reshape(tracers.shape[0], columns, levels_all)
    renewed, heat = column_step(species, mixing_k, vertical, rates, pairs, heat_map, heat_coef)
    tracers_out = renewed.reshape(tracers.shape)
    heat_cols = heat.reshape(cols_x, cols_y, levels_all)
    heat_back = lax.all_to_all(heat_cols, "lon", split_axis=2, concat_axis=1, tiled=True)
    heat_levels = jnp.transpose(heat_back, (2, 0, 1))
    state_out = stepped.at[3].set(stepped[3] + 0.5 * heat_levels)
    return (state_out, tracers_out)


def solution(mesh):
    in_specs = (
        P(None, "lon", "lat", "grp"),
        P(None, "lat", ("grp", "lon"), None),
        P(),
        P(),
        P(),
        P(),
        P(),
    )
    out_specs = (P(None, "lon", "lat", "grp"), P(None, "lat", ("grp", "lon"), None))
    return jax.shard_map(
        on_device, mesh=mesh, in_specs=in_specs, out_specs=out_specs, check_vma=False
    )
```

profile of v0, /device:TPU:192, one launch (start us, length us, event | category | flops | bytes accessed | tf_op | source)
XLA Modules:
  0.0 224.3 jit_solution(4615531750703268496)
XLA Ops:
  0.7 1.3 copy.132
  2.5 5.6 %collective-permute-start.1 = (f32[5,4,2,128]{3,0,2,1:T(8,128)}, f32[5,4,2,128]{3,0,2,1:T(8,128)}, u32[]{:S(2)}, u32[]{:S(2)}) collective-permute-start(f32[5,4,2,128]{3,0,2,1:T(8,128)} %get-tuple-element.41), channel_id=1, source_target_pairs={{0,32},{32,64},{64,96},{96,128},{128,160},{160,192},{192,224},{1,3... | collective-permute-start | bytes 61448 | tf_op jit(solution)/shard_map/ppermute | solution.py:16
  8.2 1.1 fusion.74
  9.3 13.7 %collective-permute-start.2 = (f32[5,4,32,2]{3,0,2,1:T(8,128)}, f32[5,4,32,2]{3,0,2,1:T(8,128)S(1)}, u32[]{:S(2)}, u32[]{:S(2)}) collective-permute-start(f32[5,4,32,2]{3,0,2,1:T(8,128)} %get-tuple-element.42), channel_id=1, source_target_pairs={{256,0},{512,256},{768,512},{0,768},{257,1},{513,257},{769,513},{1... | collective-permute-start | bytes 15368 | tf_op jit(solution)/shard_map/ppermute | solution.py:19
  23.0 2.5 %collective-permute-start = (f32[5,4,2,128]{3,0,2,1:T(8,128)}, f32[5,4,2,128]{3,0,2,1:T(8,128)}, u32[]{:S(2)}, u32[]{:S(2)}) collective-permute-start(f32[5,4,2,128]{3,0,2,1:T(8,128)} %get-tuple-element.40), channel_id=1, source_target_pairs={{32,0},{64,32},{96,64},{128,96},{160,128},{192,160},{224,192},{33,... | collective-permute-start | bytes 61448 | tf_op jit(solution)/shard_map/ppermute | solution.py:19
  25.4 1.9 collective-permute-start.3
  27.8 0.8 convolution_multiply_fusion.1
  28.6 0.9 convolution_multiply_fusion
  29.5 1.2 fusion.51
  31.7 0.8 reshape.108
  32.6 9.9 %all-to-all-start = ((f32[32,1,512]{2,1,0:T(1,128)}), f32[32,1,512]{2,1,0:T(1,128)S(1)}, u32[]{:S(2)}, u32[]{:S(2)}) async-start(f32[32,1,512]{2,1,0:T(1,128)} %reshape.108), calls=%async_computation | async-start | bytes 131072 | tf_op jit(solution)/shard_map/all_to_all | solution.py:115
  43.5 15.0 %collective-permute-done.2 = f32[5,4,32,2]{3,0,2,1:T(8,128)S(1)} collective-permute-done((f32[5,4,32,2]{3,0,2,1:T(8,128)}, f32[5,4,32,2]{3,0,2,1:T(8,128)S(1)}, u32[]{:S(2)}, u32[]{:S(2)}) %collective-permute-start.2) | collective-permute-done | bytes 5152 | tf_op jit(solution)/shard_map/ppermute | solution.py:19
  60.0 1.7 collective-permute-done.3
  61.7 2.3 %fusion.8 = f32[5,4,32,128]{3,0,2,1:T(8,128)S(1)} fusion(f32[5,4,32,128]{3,0,2,1:T(8,128)S(1)} %copy.132, f32[5,4,32,2]{3,0,2,1:T(8,128)} %collective-permute-done.3, f32[5,4,32,130]{3,0,2,1:T(8,128)S(1)} %constant_dynamic-update-slice_fusion.2, f32[5,4,34,128]{3,0,2,1:T(8,128)S(1)} %get-tuple-element.45, ...), kind=kOutput, calls=%fused_computation.13 | convolution fusion | flops 7045120 | bytes 4531200 | tf_op jit(solution)/shard_map/fg,gzxy->fzxy/dot_general | solution.py:42
  64.2 10.5 %collective-permute-start.6 = (f32[5,4,32,2]{3,0,2,1:T(8,128)S(1)}, f32[5,4,32,2]{3,0,2,1:T(8,128)S(1)}, u32[]{:S(2)}, u32[]{:S(2)}) collective-permute-start(f32[5,4,32,2]{3,0,2,1:T(8,128)S(1)} %get-tuple-element.38), channel_id=1, source_target_pairs={{256,0},{512,256},{768,512},{0,768},{257,1},{513,257},{769,513},{1... | collective-permute-start | bytes 15368 | tf_op jit(solution)/shard_map/ppermute | solution.py:19
  74.7 1.9 collective-permute-start.7
  76.6 1.9 collective-permute-start.4
  78.5 5.1 %collective-permute-start.5 = (f32[5,4,2,128]{3,0,2,1:T(8,128)S(1)}, f32[5,4,2,128]{3,0,2,1:T(8,128)S(1)}, u32[]{:S(2)}, u32[]{:S(2)}) collective-permute-start(f32[5,4,2,128]{3,0,2,1:T(8,128)S(1)} %get-tuple-element.37), channel_id=1, source_target_pairs={{0,32},{32,64},{64,96},{96,128},{128,160},{160,192},{192,224},{1,3... | collective-permute-start | bytes 61448 | tf_op jit(solution)/shard_map/ppermute | solution.py:16
  83.7 1.1 fusion.67
  84.8 7.3 %collective-permute-done.6 = f32[5,4,32,2]{3,0,2,1:T(8,128)S(1)} collective-permute-done((f32[5,4,32,2]{3,0,2,1:T(8,128)S(1)}, f32[5,4,32,2]{3,0,2,1:T(8,128)S(1)}, u32[]{:S(2)}, u32[]{:S(2)}) %collective-permute-start.6) | collective-permute-done | bytes 5152 | tf_op jit(solution)/shard_map/ppermute | solution.py:19
  92.1 9.8 %collective-permute-done.7 = f32[5,4,32,2]{3,0,2,1:T(8,128)S(1)} collective-permute-done((f32[5,4,32,2]{3,0,2,1:T(8,128)S(1)}, f32[5,4,32,2]{3,0,2,1:T(8,128)S(1)}, u32[]{:S(2)}, u32[]{:S(2)}) %collective-permute-start.7) | collective-permute-done | bytes 5152 | tf_op jit(solution)/shard_map/ppermute | solution.py:16
  102.0 1.6 fusion.3
  103.6 1.1 fusion.70
  105.4 25.0 %collective-permute-start.10 = (f32[5,4,32,2]{3,0,2,1:T(8,128)}, f32[5,4,32,2]{3,0,2,1:T(8,128)}, u32[]{:S(2)}, u32[]{:S(2)}) collective-permute-start(f32[5,4,32,2]{3,0,2,1:T(8,128)} %get-tuple-element.34), channel_id=1, source_target_pairs={{256,0},{512,256},{768,512},{0,768},{257,1},{513,257},{769,513},{1... | collective-permute-start | bytes 15368 | tf_op jit(solution)/shard_map/ppermute | solution.py:19
  130.4 1.9 collective-permute-start.11
  132.3 1.9 collective-permute-start.8
  134.2 5.3 %collective-permute-start.9 = (f32[5,4,2,128]{3,0,2,1:T(8,128)}, f32[5,4,2,128]{3,0,2,1:T(8,128)}, u32[]{:S(2)}, u32[]{:S(2)}) collective-permute-start(f32[5,4,2,128]{3,0,2,1:T(8,128)} %get-tuple-element.33), channel_id=1, source_target_pairs={{0,32},{32,64},{64,96},{96,128},{128,160},{160,192},{192,224},{1,3... | collective-permute-start | bytes 61448 | tf_op jit(solution)/shard_map/ppermute | solution.py:16
  139.6 1.4 fusion.68
  141.5 0.9 copy.165
  142.4 1.9 copy.158
  144.3 24.2 %collective-permute-done.10 = f32[5,4,32,2]{3,0,2,1:T(8,128)} collective-permute-done((f32[5,4,32,2]{3,0,2,1:T(8,128)}, f32[5,4,32,2]{3,0,2,1:T(8,128)}, u32[]{:S(2)}, u32[]{:S(2)}) %collective-permute-start.10) | collective-permute-done | bytes 5152 | tf_op jit(solution)/shard_map/ppermute | solution.py:19
  168.5 10.4 %collective-permute-done.11 = f32[5,4,32,2]{3,0,2,1:T(8,128)} collective-permute-done((f32[5,4,32,2]{3,0,2,1:T(8,128)}, f32[5,4,32,2]{3,0,2,1:T(8,128)}, u32[]{:S(2)}, u32[]{:S(2)}) %collective-permute-start.11) | collective-permute-done | bytes 5152 | tf_op jit(solution)/shard_map/ppermute | solution.py:16
  179.0 3.2 %fusion.7 = f32[5,4,32,128]{3,0,2,1:T(8,128)S(1)} fusion(f32[5,4,32,128]{3,0,2,1:T(8,128)S(1)} %copy-done.5, f32[5,4,32,2]{3,0,2,1:T(8,128)} %collective-permute-done.11, f32[5,4,32,2]{3,0,2,1:T(8,128)} %collective-permute-done.10, f32[5,4,2,128]{3,0,2,1:T(8,128)} %collective-permute-done.9, f32[5,4,2,128]{3,0,2,1:T(8,128)} %collective-permute-done.8, ...), kind=kOutput, calls=%fused_computation.11 | convolution fusion | flops 7782400 | bytes 1759232 | tf_op jit(solution)/shard_map/fg,gzxy->fzxy/dot_general | solution.py:42
  182.6 1.2 reshape.110
  183.8 10.0 %all-to-all-start.1 = ((f32[32,1,1536]{2,1,0:T(1,128)}), f32[32,1,1536]{2,1,0:T(1,128)S(1)}, u32[]{:S(2)}, u32[]{:S(2)}) async-start(f32[32,1,1536]{2,1,0:T(1,128)} %reshape.110), calls=%async_computation.1 | async-start | bytes 393216 | tf_op jit(solution)/shard_map/all_to_all | solution.py:105
  194.4 0.8 reduce.2
  195.7 1.3 scatter.4
  197.0 0.8 copy.160
  197.8 7.0 %all-to-all-done.1 = f32[32,1,1536]{2,1,0:T(1,128)S(1)} async-done(((f32[32,1,1536]{2,1,0:T(1,128)}), f32[32,1,1536]{2,1,0:T(1,128)S(1)}, u32[]{:S(2)}, u32[]{:S(2)}) %all-to-all-start.1) | async-done | bytes 196640 | tf_op jit(solution)/shard_map/all_to_all | solution.py:105
  204.8 1.1 reduce.3
  206.8 3.0 %copy.159 = f32[2,32,4,32,4]{4,3,2,1,0:T(8,128)} copy(f32[2,32,4,32,4]{3,1,4,2,0:T(8,128)S(1)} %slice.309) | data formatting | bytes 262144 | tf_op jit(solution)/shard_map/slice | solution.py:107
  209.9 4.9 %slice.259 = f32[2,128,128]{2,1,0:T(8,128)S(1)} reshape(f32[2,32,4,32,4]{4,3,2,1,0:T(8,128)} %copy.159) | data formatting | bytes 262144 | tf_op jit(solution)/shard_map/slice | solution.py:107
  215.0 0.8 maximum_negate_fusion
  215.9 1.8 copy.153
  217.8 1.1 copy.154
  218.8 0.8 copy.155
  219.7 1.1 copy.156
  220.7 3.6 %add_add_fusion = f32[12,32,4,128]{3,2,1,0:T(4,128)} fusion(f32[12,32,4,128]{3,2,1,0:T(4,128)S(1)} %reshape.101, f32[12,32,4,128]{3,2,1,0:T(4,128)S(1)} %copy-done.1, f32[12,32,4,1]{3,2,1,0:T(4,128)} %copy.158, f32[12,32,4,127]{3,2,1,0:T(4,128)} %bitcast.88, f32[12,32,4,127]{3,2,1,0:T(4,128)S(1)} %bitcast.87, f32[12,32,4,1]{3,2,1,0:T(4,128)S(1)} %bitcast.86, ...), kind=kLoop, calls=%fused_computation.27 | loop fusion | flops 2752512 | bytes 4128768 | tf_op jit(solution)/shard_map/add | solution.py:92
  (61 shorter events, 8.6 us)
Async XLA Ops:
  0.6 61.1 %copy-start = (f32[5,5]{1,0:T(8,128)S(1)}, f32[5,5]{1,0:T(8,128)}, u32[]{:S(2)}) copy-start(f32[5,5]{1,0:T(8,128)} %param.11) | copy-start | bytes 304
  0.6 26.7 %copy-start.8 = (s32[24,3]{0,1:T(4,128)S(1)}, s32[24,3]{0,1:T(4,128)}, u32[]{:S(2)}) copy-start(s32[24,3]{0,1:T(4,128)} %param.13) | copy-start | bytes 868
  0.7 26.7 %copy-start.1 = (f32[12,32,4,128]{3,2,1,0:T(4,128)S(1)}, f32[12,32,4,128]{3,2,1,0:T(4,128)}, u32[]{:S(2)}) copy-start(f32[12,32,4,128]{3,2,1,0:T(4,128)} %param.10) | copy-start | bytes 2359300
  2.5 25.2 %copy-start.9 = (f32[24]{0:T(128)S(1)}, f32[24]{0:T(128)}, u32[]{:S(2)}) copy-start(f32[24]{0:T(128)} %param.12) | copy-start | bytes 292
  2.5 40.0 %collective-permute-start.1 = (f32[5,4,2,128]{3,0,2,1:T(8,128)}, f32[5,4,2,128]{3,0,2,1:T(8,128)}, u32[]{:S(2)}, u32[]{:S(2)}) collective-permute-start(f32[5,4,2,128]{3,0,2,1:T(8,128)} %get-tuple-element.41), channel_id=1, source_target_pairs={{0,32},{32,64},{64,96},{96,128},{128,160},{160,192},{192,224},{1,3... | collective-permute-start | bytes 61448 | tf_op jit(solution)/shard_map/ppermute | solution.py:16
  9.3 49.2 %collective-permute-start.2 = (f32[5,4,32,2]{3,0,2,1:T(8,128)}, f32[5,4,32,2]{3,0,2,1:T(8,128)S(1)}, u32[]{:S(2)}, u32[]{:S(2)}) collective-permute-start(f32[5,4,32,2]{3,0,2,1:T(8,128)} %get-tuple-element.42), channel_id=1, source_target_pairs={{256,0},{512,256},{768,512},{0,768},{257,1},{513,257},{769,513},{1... | collective-permute-start | bytes 15368 | tf_op jit(solution)/shard_map/ppermute | solution.py:19
  23.0 36.2 %collective-permute-start = (f32[5,4,2,128]{3,0,2,1:T(8,128)}, f32[5,4,2,128]{3,0,2,1:T(8,128)}, u32[]{:S(2)}, u32[]{:S(2)}) collective-permute-start(f32[5,4,2,128]{3,0,2,1:T(8,128)} %get-tuple-element.40), channel_id=1, source_target_pairs={{32,0},{64,32},{96,64},{128,96},{160,128},{192,160},{224,192},{33,... | collective-permute-start | bytes 61448 | tf_op jit(solution)/shard_map/ppermute | solution.py:19
  25.4 36.3 %collective-permute-start.3 = (f32[5,4,32,2]{3,0,2,1:T(8,128)}, f32[5,4,32,2]{3,0,2,1:T(8,128)}, u32[]{:S(2)}, u32[]{:S(2)}) collective-permute-start(f32[5,4,32,2]{3,0,2,1:T(8,128)} %get-tuple-element.43), channel_id=1, source_target_pairs={{0,256},{256,512},{512,768},{768,0},{1,257},{257,513},{513,769},{7... | collective-permute-start | bytes 15368 | tf_op jit(solution)/shard_map/ppermute | solution.py:16
  29.5 1.2 copy-start.10
  29.5 1.2 copy-start.11
  30.7 12.6 %copy-start.6 = (f32[5,4,32,128]{3,2,1,0:T(8,128)S(1)}, f32[5,4,32,128]{3,2,1,0:T(8,128)}, u32[]{:S(2)}) copy-start(f32[5,4,32,128]{3,2,1,0:T(8,128)} %param.9) | copy-start | bytes 983044
  32.6 151.3 %all-to-all-start = ((f32[32,1,512]{2,1,0:T(1,128)}), f32[32,1,512]{2,1,0:T(1,128)S(1)}, u32[]{:S(2)}, u32[]{:S(2)}) async-start(f32[32,1,512]{2,1,0:T(1,128)} %reshape.108), calls=%async_computation | async-start | bytes 131072 | tf_op jit(solution)/shard_map/all_to_all | solution.py:115
  64.2 27.9 %collective-permute-start.6 = (f32[5,4,32,2]{3,0,2,1:T(8,128)S(1)}, f32[5,4,32,2]{3,0,2,1:T(8,128)S(1)}, u32[]{:S(2)}, u32[]{:S(2)}) collective-permute-start(f32[5,4,32,2]{3,0,2,1:T(8,128)S(1)} %get-tuple-element.38), channel_id=1, source_target_pairs={{256,0},{512,256},{768,512},{0,768},{257,1},{513,257},{769,513},{1... | collective-permute-start | bytes 15368 | tf_op jit(solution)/shard_map/ppermute | solution.py:19
  74.7 27.3 %collective-permute-start.7 = (f32[5,4,32,2]{3,0,2,1:T(8,128)S(1)}, f32[5,4,32,2]{3,0,2,1:T(8,128)S(1)}, u32[]{:S(2)}, u32[]{:S(2)}) collective-permute-start(f32[5,4,32,2]{3,0,2,1:T(8,128)S(1)} %get-tuple-element.39), channel_id=1, source_target_pairs={{0,256},{256,512},{512,768},{768,0},{1,257},{257,513},{513,769},{7... | collective-permute-start | bytes 15368 | tf_op jit(solution)/shard_map/ppermute | solution.py:16
  76.6 25.4 %collective-permute-start.4 = (f32[5,4,2,128]{3,0,2,1:T(8,128)S(1)}, f32[5,4,2,128]{3,0,2,1:T(8,128)S(1)}, u32[]{:S(2)}, u32[]{:S(2)}) collective-permute-start(f32[5,4,2,128]{3,0,2,1:T(8,128)S(1)} %get-tuple-element.36), channel_id=1, source_target_pairs={{32,0},{64,32},{96,64},{128,96},{160,128},{192,160},{224,192},{33,... | collective-permute-start | bytes 61448 | tf_op jit(solution)/shard_map/ppermute | solution.py:19
  78.5 23.5 %collective-permute-start.5 = (f32[5,4,2,128]{3,0,2,1:T(8,128)S(1)}, f32[5,4,2,128]{3,0,2,1:T(8,128)S(1)}, u32[]{:S(2)}, u32[]{:S(2)}) collective-permute-start(f32[5,4,2,128]{3,0,2,1:T(8,128)S(1)} %get-tuple-element.37), channel_id=1, source_target_pairs={{0,32},{32,64},{64,96},{96,128},{128,160},{160,192},{192,224},{1,3... | collective-permute-start | bytes 61448 | tf_op jit(solution)/shard_map/ppermute | solution.py:16
  83.7 18.3 %copy-start.7 = (f32[5,4,32,128]{3,2,1,0:T(8,128)S(1)}, f32[5,4,32,128]{3,2,1,0:T(8,128)}, u32[]{:S(2)}) copy-start(f32[5,4,32,128]{3,2,1,0:T(8,128)} %param.9) | copy-start | bytes 983044
  103.6 36.0 %copy-start.4 = (f32[5,4,32,128]{3,0,2,1:T(8,128)}, f32[5,4,32,128]{3,0,2,1:T(8,128)S(1)}, u32[]{:S(2)}) copy-start(f32[5,4,32,128]{3,0,2,1:T(8,128)S(1)} %fusion.3) | copy-start | bytes 983044
  105.4 63.2 %collective-permute-start.10 = (f32[5,4,32,2]{3,0,2,1:T(8,128)}, f32[5,4,32,2]{3,0,2,1:T(8,128)}, u32[]{:S(2)}, u32[]{:S(2)}) collective-permute-start(f32[5,4,32,2]{3,0,2,1:T(8,128)} %get-tuple-element.34), channel_id=1, source_target_pairs={{256,0},{512,256},{768,512},{0,768},{257,1},{513,257},{769,513},{1... | collective-permute-start | bytes 15368 | tf_op jit(solution)/shard_map/ppermute | solution.py:19
  130.4 48.6 %collective-permute-start.11 = (f32[5,4,32,2]{3,0,2,1:T(8,128)}, f32[5,4,32,2]{3,0,2,1:T(8,128)}, u32[]{:S(2)}, u32[]{:S(2)}) collective-permute-start(f32[5,4,32,2]{3,0,2,1:T(8,128)} %get-tuple-element.35), channel_id=1, source_target_pairs={{0,256},{256,512},{512,768},{768,0},{1,257},{257,513},{513,769},{7... | collective-permute-start | bytes 15368 | tf_op jit(solution)/shard_map/ppermute | solution.py:16
  132.3 46.7 %collective-permute-start.8 = (f32[5,4,2,128]{3,0,2,1:T(8,128)}, f32[5,4,2,128]{3,0,2,1:T(8,128)}, u32[]{:S(2)}, u32[]{:S(2)}) collective-permute-start(f32[5,4,2,128]{3,0,2,1:T(8,128)} %get-tuple-element.32), channel_id=1, source_target_pairs={{32,0},{64,32},{96,64},{128,96},{160,128},{192,160},{224,192},{33,... | collective-permute-start | bytes 61448 | tf_op jit(solution)/shard_map/ppermute | solution.py:19
  134.2 44.7 %collective-permute-start.9 = (f32[5,4,2,128]{3,0,2,1:T(8,128)}, f32[5,4,2,128]{3,0,2,1:T(8,128)}, u32[]{:S(2)}, u32[]{:S(2)}) collective-permute-start(f32[5,4,2,128]{3,0,2,1:T(8,128)} %get-tuple-element.33), channel_id=1, source_target_pairs={{0,32},{32,64},{64,96},{96,128},{128,160},{160,192},{192,224},{1,3... | collective-permute-start | bytes 61448 | tf_op jit(solution)/shard_map/ppermute | solution.py:16
  141.5 37.4 %copy-start.5 = (f32[5,4,32,128]{3,0,2,1:T(8,128)S(1)}, f32[5,4,32,128]{3,0,2,1:T(8,128)}, u32[]{:S(2)}) copy-start(f32[5,4,32,128]{3,0,2,1:T(8,128)} %copy-done.4) | copy-start | bytes 983044
  183.8 21.0 %all-to-all-start.1 = ((f32[32,1,1536]{2,1,0:T(1,128)}), f32[32,1,1536]{2,1,0:T(1,128)S(1)}, u32[]{:S(2)}, u32[]{:S(2)}) async-start(f32[32,1,1536]{2,1,0:T(1,128)} %reshape.110), calls=%async_computation.1 | async-start | bytes 393216 | tf_op jit(solution)/shard_map/all_to_all | solution.py:105
  214.9 5.8 %copy-start.2 = (f32[12,128,1]{2,1,0:T(8,128)S(1)}, f32[12,128,1]{2,1,0:T(8,128)}, u32[]{:S(2)}) copy-start(f32[12,128,1]{2,1,0:T(8,128)} %get-tuple-element.28) | copy-start | bytes 18436
  215.7 5.0 %copy-start.3 = (f32[12,128,127]{2,1,0:T(8,128)S(1)}, f32[12,128,127]{2,1,0:T(8,128)}, u32[]{:S(2)}) copy-start(f32[12,128,127]{2,1,0:T(8,128)} %get-tuple-element.30) | copy-start | bytes 2340868
where the time goes:
time: 225 us; the launch traced here: 224 us
  starting transfers between devices  97.2 us (43%)
  waiting for transfers between devices  76.2 us (34%)
  local copies, waits for them, and re-layouts  32.5 us (14%)
  matrix products  10.7 us (5%)
  other arithmetic  6.48 us (3%)
    ppermute x6, starting transfers between devices, extended(): lax.ppermute(lax.slice_in_dim(block, 0, width, axis=dim), axis, backward)  55.5 us
    ppermute x6, waiting for transfers between devices, extended(): lax.ppermute(lax.slice_in_dim(block, 0, width, axis=dim), axis, backward)  47.2 us
    ppermute x6, waiting for transfers between devices, extended(): lax.ppermute(lax.slice_in_dim(block, block.shape[dim] - width, None, axis...  22 us
    ppermute x6, starting transfers between devices, extended(): lax.ppermute(lax.slice_in_dim(block, block.shape[dim] - width, None, axis...  21.8 us
    all_to_all x1, starting transfers between devices, on_device(): lax.all_to_all(outgoing, 'lon', split_axis=2, concat_axis=3, tiled=True)  9.96 us
    all_to_all x1, starting transfers between devices, on_device(): lax.all_to_all(heat_cols, 'lon', split_axis=2, concat_axis=1, tiled=True)  9.95 us
    slice x3, local copies, waits for them, and re-layouts, on_device(): higher, lower = clamped(regrouped[0:2], 2)  7.93 us
    all_to_all x1, waiting for transfers between devices, on_device(): lax.all_to_all(outgoing, 'lon', split_axis=2, concat_axis=3, tiled=True)  7.03 us
  transfers between devices with their start and end apart: 14, of which 8 were waited for; matrix products, arithmetic and copies ran while one was open for 13% of the time, Pallas kernels for 0%

commit v1 on v0

v1 whole, which is shorter than its diff:
```python
import jax
import jax.numpy as jnp
from jax import lax
from jax.experimental import pallas as pl
from jax.experimental.pallas import tpu as pltpu
from jax.sharding import PartitionSpec as P

FIELDS = 5
LEVELS = 4
PLANES = FIELDS * LEVELS
ROWS = 32
LANES = 128
HALO = 6
BAND = 8
PEERS = 32
SLOTS = 16
SPECIES = 12
REACTIONS = 24


def lane_index(rows):
    return lax.broadcasted_iota(jnp.int32, (rows, LANES), 1)


def pack_kernel(state_ref, far_ref, near_ref):
    odd = lax.rem(lax.axis_index("grp"), 2) == 1
    lanes = lane_index(ROWS)
    left = jnp.zeros((ROWS, LANES), jnp.float32)
    right = jnp.zeros((ROWS, LANES), jnp.float32)
    for plane in range(PLANES):
        tile = state_ref[plane]
        keep = lanes >= HALO * plane
        left = jnp.where(keep, pltpu.roll(tile, HALO * plane, 1) if plane else tile, left)
        right = jnp.where(keep, pltpu.roll(tile, HALO * plane + HALO, 1), right)
    far_ref[...] = jnp.where(odd, right, left)
    near_ref[...] = jnp.where(odd, left, right)


def regroup(chunks):
    lanes = lane_index(ROWS)
    width = LANES // 4
    out = []
    for j in range(4):
        total = None
        for i in range(4):
            turn = (width * (i - j)) % LANES
            moved = pltpu.roll(chunks[i], turn, 1) if turn else chunks[i]
            total = moved if total is None else jnp.where(lanes >= width * i, moved, total)
        out.append(total)
    return out


def chem_kernel(rates_ref, pairs_ref, map_ref, coef_ref, q_ref, pre_ref, heat_ref, heat_sc, turn_sc):
    pre_ref[...] = q_ref[...]
    heat_sc[...] = jnp.zeros_like(heat_sc)

    def weight(species):
        return coef_ref[map_ref[species]]

    def react(r, carry):
        a, b, p = pairs_ref[r, 0], pairs_ref[r, 1], pairs_ref[r, 2]
        rate = rates_ref[r] * q_ref[a] * q_ref[b]
        heat_sc[...] += (weight(p) - weight(a) - weight(b)) * rate
        pre_ref[p] += rate
        pre_ref[a] -= rate
        pre_ref[b] -= rate
        return carry

    lax.fori_loop(0, REACTIONS, react, 0)
    ordered = jnp.concatenate([heat_sc[pl.ds(y, ROWS, stride=4), :] for y in range(4)], 0)
    turn_sc[...] = jnp.transpose(ordered)
    chunks = [turn_sc[pl.ds(level, PEERS, stride=4), :] for level in range(4)]
    for y, block in enumerate(regroup(chunks)):
        heat_ref[y] = block


def rk_kernel(
    coupling_ref, state_ref, low_ref, high_ref, far_ref, near_ref, under_ref, over_ref, heat_ref,
    out_ref, send_ref, sa, sb, ta, tb, ua, ub, turn_sc,
):
    odd = lax.rem(lax.axis_index("grp"), 2) == 1
    lat = lax.axis_index("lat")
    has_low = lat > 0
    has_high = lat < lax.axis_size("lat") - 1
    base = 16

    far = jnp.concatenate([under_ref[0:BAND], far_ref[...], over_ref[0:BAND]], 0)
    near = jnp.concatenate([under_ref[BAND:], near_ref[...], over_ref[BAND:]], 0)
    left = jnp.where(odd, near, far)
    right = jnp.where(odd, far, near)
    span = ROWS + 2 * BAND
    lanes = lane_index(span)
    for plane in range(PLANES):
        sa[plane, base - BAND : base, :] = low_ref[plane]
        sa[plane, base : base + ROWS, :] = state_ref[plane]
        sa[plane, base + ROWS : base + ROWS + BAND, :] = high_ref[plane]
        beyond = pltpu.roll(right, (-HALO * plane) % LANES, 1) if plane else right
        before = pltpu.roll(left, (LANES - HALO - HALO * plane) % LANES, 1)
        edge = jnp.where(lanes >= LANES - HALO, before, 0.0)
        sb[plane, base - BAND : base + ROWS + BAND, :] = jnp.where(lanes < HALO, beyond, edge)

    lane8 = lane_index(8)
    weights = [
        [coupling_ref[f, g] + (0.6 if f == g else 0.0) for g in range(FIELDS)] for f in range(FIELDS)
    ]

    def apply(a_ref, b_ref, z, row, both):
        centers_a = [a_ref[f * LEVELS + z, row : row + 8, :] for f in range(FIELDS)]
        centers_b = [b_ref[f * LEVELS + z, row : row + 8, :] for f in range(FIELDS)]

        def along_lanes(f):
            moved = {}
            for j in (1, 2, -1, -2):
                ra = pltpu.roll(centers_a[f], -j % LANES, 1)
                rb = pltpu.roll(centers_b[f], -j % LANES, 1)
                inner = lane8 < LANES - j if j > 0 else lane8 >= -j
                moved[j] = (jnp.where(inner, ra, rb), jnp.where(inner, rb, ra) if both else None)
            return moved

        result = []
        for f in range(FIELDS):
            moved = along_lanes(f)
            pieces = []
            for part, ref, centers in ((0, a_ref, centers_a), (1, b_ref, centers_b)):
                if part == 1 and not both:
                    break
                x = {j: ref[f * LEVELS + z, row + j : row + j + 8, :] for j in (1, 2, -1, -2)}
                total = -0.1 * (x[1] + moved[1][part]) + 0.3 * (x[-1] + moved[-1][part])
                total = total + 0.025 * ((x[2] - x[-2]) + (moved[2][part] - moved[-2][part]))
                for g in range(FIELDS):
                    total = total + weights[f][g] * centers[g]
                pieces.append(total)
            result.append(pieces)
        return result

    first, last = base - BAND, base + ROWS

    def masked(value, row):
        if row == first:
            return jnp.where(has_low, value, 0.0)
        if row == last:
            return jnp.where(has_high, value, 0.0)
        return value

    def stage_one(z, carry):
        for row in range(first, last + 8, 8):
            for f, (a, b) in enumerate(apply(sa, sb, z, row, True)):
                ta[f * LEVELS + z, row : row + 8, :] = masked(a, row)
                tb[f * LEVELS + z, row : row + 8, :] = masked(b, row)
        return carry

    def stage_two(z, carry):
        for row in range(first, last + 8, 8):
            for f, (a, b) in enumerate(apply(ta, tb, z, row, True)):
                plane = f * LEVELS + z
                ua[plane, row : row + 8, :] = masked(0.75 * sa[plane, row : row + 8, :] + 0.25 * a, row)
                ub[plane, row : row + 8, :] = masked(0.75 * sb[plane, row : row + 8, :] + 0.25 * b, row)
        return carry

    def stage_three(z, carry):
        for row in range(base, last, 8):
            for f, (a,) in enumerate(apply(ua, ub, z, row, False)):
                plane = f * LEVELS + z
                value = sa[plane, row : row + 8, :] * (1.0 / 3.0) + (2.0 / 3.0) * a
                out_ref[plane, row - base : row - base + 8, :] = value
        return carry

    lax.fori_loop(0, LEVELS, stage_one, 0)
    lax.fori_loop(0, LEVELS, stage_two, 0)
    lax.fori_loop(0, LEVELS, stage_three, 0)

    for f in range(3):
        plane = jnp.concatenate([out_ref[f * LEVELS + z] for z in range(LEVELS)], 0)
        turn_sc[f] = jnp.transpose(plane)
        chunks = [turn_sc[f, pl.ds(y, PEERS, stride=4), :] for y in range(4)]
        for level, block in enumerate(regroup(chunks)):
            send_ref[pl.ds(4 * f + level, PEERS, stride=SLOTS), :] = block
    for y in range(4):
        send_ref[pl.ds(12 + y, PEERS, stride=SLOTS), :] = heat_ref[y]


def final_kernel(recv_ref, temp_ref, q_ref, pre_ref, temp_out_ref, q_out_ref, turn_sc, wind_sc):
    for y in range(4):
        turn_sc[pl.ds(y, PEERS, stride=4), :] = recv_ref[pl.ds(12 + y, PEERS, stride=SLOTS), :]
    temp_out_ref[0] = temp_ref[0] + 0.5 * jnp.transpose(turn_sc[...])
    for f in range(3):
        for level in range(4):
            turn_sc[pl.ds(level, PEERS, stride=4), :] = recv_ref[pl.ds(4 * f + level, PEERS, stride=SLOTS), :]
        columns = jnp.transpose(turn_sc[...])
        for y in range(4):
            wind_sc[f, pl.ds(y, ROWS, stride=4), :] = columns[y * ROWS : (y + 1) * ROWS]

    chunk = 32
    lanes = lane_index(chunk)

    def clamped(value):
        higher = jnp.where(lanes == LANES - 1, value, pltpu.roll(value, LANES - 1, 1))
        lower = jnp.where(lanes == 0, value, pltpu.roll(value, 1, 1))
        return higher, lower

    for start in range(0, 128, chunk):
        rows = slice(start, start + chunk)
        shear = None
        for f in range(2):
            higher, lower = clamped(wind_sc[f, rows, :])
            square = (higher - lower) * (higher - lower)
            shear = square if shear is None else shear + square
        mixing = 0.2 * shear / (1.0 + shear)
        vertical = wind_sc[2, rows, :]
        speed = 0.4 * vertical / (1.0 + jnp.abs(vertical))
        up = mixing - jnp.minimum(speed, 0.0)
        down = mixing + jnp.maximum(speed, 0.0)
        for s in range(SPECIES):
            value = q_ref[s, rows, :]
            higher, lower = clamped(value)
            q_out_ref[s, rows, :] = pre_ref[s, rows, :] + (up * (higher - value) - down * (value - lower))


VMEM = pl.BlockSpec(memory_space=pltpu.VMEM)
SMEM = pl.BlockSpec(memory_space=pltpu.SMEM)


def shape(*dims):
    return jax.ShapeDtypeStruct(dims, jnp.float32)


def cost(flops, data):
    return pl.CostEstimate(flops=flops, bytes_accessed=data, transcendentals=0)


def on_device(state, tracers, coupling, rates, pairs, heat_map, heat_coef):
    planes = state.reshape(PLANES, ROWS, LANES)
    q = tracers.reshape(SPECIES, 128, 128)

    far, near = pl.pallas_call(
        pack_kernel,
        out_shape=(shape(ROWS, LANES), shape(ROWS, LANES)),
        in_specs=[VMEM],
        out_specs=(VMEM, VMEM),
        cost_estimate=cost(1000000, 400000),
    )(planes)
    far_in = lax.ppermute(far, "grp", [(0, 3), (3, 0), (1, 2), (2, 1)])
    near_in = lax.ppermute(near, "grp", [(0, 1), (1, 0), (2, 3), (3, 2)])
    count = lax.axis_size("lat")
    up = [(i, i + 1) for i in range(count - 1)]
    down = [(i + 1, i) for i in range(count - 1)]
    low = lax.ppermute(planes[:, ROWS - BAND :], "lat", up)
    high = lax.ppermute(planes[:, :BAND], "lat", down)

    pre, heat = pl.pallas_call(
        chem_kernel,
        out_shape=(shape(SPECIES, 128, 128), shape(4, PEERS, LANES)),
        in_specs=[SMEM, SMEM, SMEM, SMEM, VMEM],
        out_specs=(VMEM, VMEM),
        scratch_shapes=[pltpu.VMEM((128, 128), jnp.float32), pltpu.VMEM((128, 128), jnp.float32)],
        cost_estimate=cost(10000000, 2000000),
    )(rates, pairs, heat_map, heat_coef, q)

    under = lax.ppermute(jnp.concatenate([far_in[ROWS - BAND :], near_in[ROWS - BAND :]], 0), "lat", up)
    over = lax.ppermute(jnp.concatenate([far_in[:BAND], near_in[:BAND]], 0), "lat", down)

    extended = pltpu.VMEM((PLANES, 64, LANES), jnp.float32)
    stepped, send = pl.pallas_call(
        rk_kernel,
        out_shape=(shape(PLANES, ROWS, LANES), shape(PEERS * SLOTS, LANES)),
        in_specs=[SMEM] + [VMEM] * 8,
        out_specs=(VMEM, VMEM),
        scratch_shapes=[extended] * 6 + [pltpu.VMEM((3, 128, 128), jnp.float32)],
        cost_estimate=cost(20000000, 1500000),
    )(coupling, planes, low, high, far_in, near_in, under, over, heat)

    received = lax.all_to_all(
        send.reshape(PEERS, SLOTS, LANES), "lon", split_axis=0, concat_axis=0, tiled=True
    )
    temperature = pl.BlockSpec((1, 128, 128), lambda i: (3, 0, 0))
    whole = pl.BlockSpec((SPECIES, 128, 128), lambda i: (0, 0, 0))
    state_out, q_out = pl.pallas_call(
        final_kernel,
        grid=(1,),
        out_shape=(shape(FIELDS, 128, 128), shape(SPECIES, 128, 128)),
        in_specs=[pl.BlockSpec((PEERS * SLOTS, LANES), lambda i: (0, 0)), temperature, whole, whole],
        out_specs=(temperature, whole),
        scratch_shapes=[pltpu.VMEM((128, 128), jnp.float32), pltpu.VMEM((3, 128, 128), jnp.float32)],
        input_output_aliases={1: 0},
        cost_estimate=cost(10000000, 2500000),
    )(received.reshape(PEERS * SLOTS, LANES), stepped.reshape(FIELDS, 128, 128), q, pre)
    return state_out.reshape(state.shape), q_out.reshape(tracers.shape)


def solution(mesh):
    in_specs = (
        P(None, "lon", "lat", "grp"),
        P(None, "lat", ("grp", "lon"), None),
        P(),
        P(),
        P(),
        P(),
        P(),
    )
    out_specs = (P(None, "lon", "lat", "grp"), P(None, "lat", ("grp", "lon"), None))
    return jax.shard_map(
        on_device, mesh=mesh, in_specs=in_specs, out_specs=out_specs, check_vma=False
    )
```

time: 225 us -> 71.7 us (0.32)
  the two profiles are of different devices: /device:TPU:192 before, /device:TPU:64 now
where the time goes in v1:
time: 71.7 us; the launch traced here: 71.3 us
  starting transfers between devices  32.1 us (45%)
  blocking collectives  22.2 us (31%)
  Pallas kernels  14 us (20%)
  local copies, waits for them, and re-layouts  1.96 us (3%)
  between operations  0.79 us (1%)
    all_to_all x1, blocking collectives, on_device(): lax.all_to_all(send.reshape(PEERS, SLOTS, LANES), 'lon', split_axis=0, co...  22.2 us
    ppermute x1, starting transfers between devices, on_device(): far_in = lax.ppermute(far, 'grp', [(0, 3), (3, 0), (1, 2), (2, 1)])  17.9 us
    pallas_call x1, Pallas kernels, on_device(): pl.pallas_call(rk_kernel, out_shape=(shape(PLANES, ROWS, LANES), shape(PE...  6.13 us
    ppermute x1, starting transfers between devices, on_device(): low = lax.ppermute(planes[:, ROWS - BAND:], 'lat', up)  3.38 us
    ppermute x1, starting transfers between devices, on_device(): lax.ppermute(jnp.concatenate([far_in[ROWS - BAND:], near_in[ROWS - BAND:]...  3.37 us
    pallas_call x1, Pallas kernels, on_device(): pl.pallas_call(final_kernel, grid=(1,), out_shape=(shape(FIELDS, 128, 128...  3.08 us
    pallas_call x1, Pallas kernels, on_device(): pl.pallas_call(chem_kernel, out_shape=(shape(SPECIES, 128, 128), shape(4,...  2.92 us
    ppermute x1, starting transfers between devices, on_device(): near_in = lax.ppermute(near, 'grp', [(0, 1), (1, 0), (2, 3), (3, 2)])  2.58 us
  transfers between devices with their start and end apart: 6, of which 1 were waited for; matrix products, arithmetic and copies ran while one was open for 1% of the time, Pallas kernels for 4%

profile of v1, /device:TPU:64, one launch (start us, length us, event | category | flops | bytes accessed | tf_op | source)
XLA Modules:
  0.0 71.3 jit_solution(17498271578832468727)
XLA Ops:
  0.6 0.0 copy-start
  0.6 1.9 %shard_map.86 = (f32[32,128]{1,0:T(8,128)}, f32[32,128]{1,0:T(8,128)}) custom-call(f32[20,32,128]{2,1,0:T(8,128)} %bitcast.9), custom_call_target="tpu_custom_call" | custom-call | flops 1000000 | bytes 400000 | tf_op jit(solution)/shard_map/pallas_call | solution.py:235
  2.5 17.9 %collective-permute-start.2 = (f32[32,128]{1,0:T(8,128)}, f32[32,128]{1,0:T(8,128)S(1)}, u32[]{:S(2)}, u32[]{:S(2)}) collective-permute-start(f32[32,128]{1,0:T(8,128)} %get-tuple-element.10), channel_id=1, source_target_pairs={{0,768},{768,0},{256,512},{512,256},{1,769},{769,1},{257,513},{513... | collective-permute-start | bytes 49160 | tf_op jit(solution)/shard_map/ppermute | solution.py:242
  20.4 2.6 %collective-permute-start.3 = (f32[32,128]{1,0:T(8,128)}, f32[32,128]{1,0:T(8,128)S(1)}, u32[]{:S(2)}, u32[]{:S(2)}) collective-permute-start(f32[32,128]{1,0:T(8,128)} %get-tuple-element.11), channel_id=1, source_target_pairs={{0,256},{256,0},{512,768},{768,512},{1,257},{257,1},{513,769},{769... | collective-permute-start | bytes 49160 | tf_op jit(solution)/shard_map/ppermute | solution.py:243
  23.0 0.0 copy-done
  23.0 2.5 %collective-permute-start.1 = (f32[20,8,128]{2,1,0:T(8,128)S(1)}, f32[20,8,128]{2,1,0:T(8,128)S(1)}, u32[]{:S(2)}, u32[]{:S(2)}) collective-permute-start(f32[20,8,128]{2,1,0:T(8,128)S(1)} %get-tuple-element.18), channel_id=1, source_target_pairs={{32,0},{64,32},{96,64},{128,96},{160,128},{192,160},{224,192},{33,... | collective-permute-start | bytes 245768 | tf_op jit(solution)/shard_map/ppermute | solution.py:248
  25.5 3.4 %collective-permute-start = (f32[20,8,128]{2,1,0:T(8,128)S(1)}, f32[20,8,128]{2,1,0:T(8,128)S(1)}, u32[]{:S(2)}, u32[]{:S(2)}) collective-permute-start(f32[20,8,128]{2,1,0:T(8,128)S(1)} %get-tuple-element.19), channel_id=1, source_target_pairs={{0,32},{32,64},{64,96},{96,128},{128,160},{160,192},{192,224},{1,3... | collective-permute-start | bytes 245768 | tf_op jit(solution)/shard_map/ppermute | solution.py:247
  28.9 0.0 collective-permute-done.2.far_ref
  28.9 0.0 copy-start.3
  28.9 0.0 collective-permute-done.3.near_ref
  28.9 0.0 copy-start.4
  29.0 0.5 copy-done.3
  29.5 0.0 copy-done.4
  29.5 3.4 %collective-permute-start.4 = (f32[16,128]{1,0:T(8,128)S(1)}, f32[16,128]{1,0:T(8,128)S(1)}, u32[]{:S(2)}, u32[]{:S(2)}) collective-permute-start(f32[16,128]{1,0:T(8,128)S(1)} %pad_maximum_fusion), channel_id=1, source_target_pairs={{0,32},{32,64},{64,96},{96,128},{128,160},{160,192},{192,224},{1,3... | collective-permute-start | bytes 24584 | tf_op jit(solution)/shard_map/ppermute | solution.py:259
  32.9 0.0 copy-start.7
  32.9 2.5 %collective-permute-start.5 = (f32[16,128]{1,0:T(8,128)S(1)}, f32[16,128]{1,0:T(8,128)S(1)}, u32[]{:S(2)}, u32[]{:S(2)}) collective-permute-start(f32[16,128]{1,0:T(8,128)S(1)} %pad_maximum_fusion.1), channel_id=1, source_target_pairs={{32,0},{64,32},{96,64},{128,96},{160,128},{192,160},{224,192},{33,... | collective-permute-start | bytes 24584 | tf_op jit(solution)/shard_map/ppermute | solution.py:260
  35.4 0.0 copy-done.7
  35.4 0.7 copy.10.pairs_ref
  36.1 2.9 %shard_map.87 = (f32[12,128,128]{2,1,0:T(8,128)}, f32[4,32,128]{2,1,0:T(8,128)}) custom-call(f32[24]{0:T(128)} %rates_ref.1, s32[24,3]{1,0:T(8,128)} %copy.10.pairs_ref, s32[12]{0:T(128)} %map_ref.1, f32[4]{0:T(128)} %coef_ref.1, f32[12,128,128]{2,1,0:T(8,128)} %bitcast.7), custom_call_target="tpu_custom_call" | custom-call | flops 10000000 | bytes 2000000 | tf_op jit(solution)/shard_map/pallas_call | solution.py:250
  39.0 0.0 collective-permute-done.4.under_ref
  39.0 0.0 copy-start.5
  39.0 0.1 collective-permute-done.5.over_ref
  39.2 0.0 copy-start.6
  39.2 0.0 collective-permute-done.1.high_ref
  39.2 0.0 copy-start.1
  39.2 0.0 collective-permute-done.low_ref
  39.2 0.0 copy-start.2
  39.2 0.4 copy-done.5
  39.6 0.1 copy-done.6
  39.8 0.0 copy-done.1
  39.8 0.0 copy-done.2
  39.8 6.1 %shard_map.88 = (f32[20,32,128]{2,1,0:T(8,128)}, f32[512,128]{1,0:T(8,128)}) custom-call(f32[5,5]{1,0:T(8,128)} %coupling_ref.1, f32[20,32,128]{2,1,0:T(8,128)} %bitcast.10, f32[20,8,128]{2,1,0:T(8,128)} %copy-done.2, f32[20,8,128]{2,1,0:T(8,128)} %copy-done.1, f32[32,128]{1,0:T(8,128)} %copy-done.3, f32[32,128]{1,0:T(8,128)} %copy-done.4, ...), custom_call_target="tpu_custom_call" | custom-call | flops 20000000 | bytes 1500000 | tf_op jit(solution)/shard_map/pallas_call | solution.py:263
  46.0 22.2 %all_to_all.5 = f32[32,16,128]{2,1,0:T(8,128)} all-to-all(f32[32,16,128]{2,1,0:T(8,128)} %bitcast.15), channel_id=1, replica_groups=mesh['grp'=4,'lat'=8,'lon'=32] {'lon'}, dimensions={0} | all-to-all | bytes 524288 | tf_op jit(solution)/shard_map/all_to_all | solution.py:272
  68.2 3.1 %shard_map.89 = (f32[5,128,128]{2,1,0:T(8,128)}, f32[12,128,128]{2,1,0:T(8,128)}) custom-call(f32[512,128]{1,0:T(8,128)} %bitcast.12, f32[5,128,128]{2,1,0:T(8,128)} %bitcast.13, f32[12,128,128]{2,1,0:T(8,128)} %bitcast.8, f32[12,128,128]{2,1,0:T(8,128)} %get-tuple-element.15.pre_ref), custom_call_target="tpu_custom_call", output_to_operand_aliasing={{0}: (1, {})} | custom-call | flops 10000000 | bytes 2500000 | tf_op jit(solution)/shard_map/pallas_call | solution.py:277
  (5 shorter events, 0.0 us)
Async XLA Ops:
  0.6 22.4 %copy-start = (f32[5,4,32,128]{3,2,1,0:T(8,128)S(1)}, f32[5,4,32,128]{3,2,1,0:T(8,128)}, u32[]{:S(2)}) copy-start(f32[5,4,32,128]{3,2,1,0:T(8,128)} %param.7) | copy-start | bytes 983044
  2.5 26.4 %collective-permute-start.2 = (f32[32,128]{1,0:T(8,128)}, f32[32,128]{1,0:T(8,128)S(1)}, u32[]{:S(2)}, u32[]{:S(2)}) collective-permute-start(f32[32,128]{1,0:T(8,128)} %get-tuple-element.10), channel_id=1, source_target_pairs={{0,768},{768,0},{256,512},{512,256},{1,769},{769,1},{257,513},{513... | collective-permute-start | bytes 49160 | tf_op jit(solution)/shard_map/ppermute | solution.py:242
  20.4 8.5 %collective-permute-start.3 = (f32[32,128]{1,0:T(8,128)}, f32[32,128]{1,0:T(8,128)S(1)}, u32[]{:S(2)}, u32[]{:S(2)}) collective-permute-start(f32[32,128]{1,0:T(8,128)} %get-tuple-element.11), channel_id=1, source_target_pairs={{0,256},{256,0},{512,768},{768,512},{1,257},{257,1},{513,769},{769... | collective-permute-start | bytes 49160 | tf_op jit(solution)/shard_map/ppermute | solution.py:243
  23.0 16.1 %collective-permute-start.1 = (f32[20,8,128]{2,1,0:T(8,128)S(1)}, f32[20,8,128]{2,1,0:T(8,128)S(1)}, u32[]{:S(2)}, u32[]{:S(2)}) collective-permute-start(f32[20,8,128]{2,1,0:T(8,128)S(1)} %get-tuple-element.18), channel_id=1, source_target_pairs={{32,0},{64,32},{96,64},{128,96},{160,128},{192,160},{224,192},{33,... | collective-permute-start | bytes 245768 | tf_op jit(solution)/shard_map/ppermute | solution.py:248
  25.5 13.7 %collective-permute-start = (f32[20,8,128]{2,1,0:T(8,128)S(1)}, f32[20,8,128]{2,1,0:T(8,128)S(1)}, u32[]{:S(2)}, u32[]{:S(2)}) collective-permute-start(f32[20,8,128]{2,1,0:T(8,128)S(1)} %get-tuple-element.19), channel_id=1, source_target_pairs={{0,32},{32,64},{64,96},{96,128},{128,160},{160,192},{192,224},{1,3... | collective-permute-start | bytes 245768 | tf_op jit(solution)/shard_map/ppermute | solution.py:247
  28.9 0.6 copy-start.3
  28.9 0.6 copy-start.4
  29.5 9.5 %collective-permute-start.4 = (f32[16,128]{1,0:T(8,128)S(1)}, f32[16,128]{1,0:T(8,128)S(1)}, u32[]{:S(2)}, u32[]{:S(2)}) collective-permute-start(f32[16,128]{1,0:T(8,128)S(1)} %pad_maximum_fusion), channel_id=1, source_target_pairs={{0,32},{32,64},{64,96},{96,128},{128,160},{160,192},{192,224},{1,3... | collective-permute-start | bytes 24584 | tf_op jit(solution)/shard_map/ppermute | solution.py:259
  32.9 2.5 %copy-start.7 = (s32[24,3]{0,1:T(4,128)S(1)}, s32[24,3]{0,1:T(4,128)}, u32[]{:S(2)}) copy-start(s32[24,3]{0,1:T(4,128)} %param.11) | copy-start | bytes 868
  32.9 6.2 %collective-permute-start.5 = (f32[16,128]{1,0:T(8,128)S(1)}, f32[16,128]{1,0:T(8,128)S(1)}, u32[]{:S(2)}, u32[]{:S(2)}) collective-permute-start(f32[16,128]{1,0:T(8,128)S(1)} %pad_maximum_fusion.1), channel_id=1, source_target_pairs={{32,0},{64,32},{96,64},{128,96},{160,128},{192,160},{224,192},{33,... | collective-permute-start | bytes 24584 | tf_op jit(solution)/shard_map/ppermute | solution.py:260
  39.0 0.6 copy-start.5
  39.2 0.6 copy-start.6
  39.2 0.6 copy-start.1
  39.2 0.7 copy-start.2

commit v2 on v1

--- a/solution.py
+++ b/solution.py
@@ -12,6 +12,7 @@
 LANES = 128
 HALO = 6
 BAND = 8
+SPAN = ROWS + 2 * BAND
 PEERS = 32
 SLOTS = 16
 SPECIES = 12
@@ -22,18 +23,18 @@
     return lax.broadcasted_iota(jnp.int32, (rows, LANES), 1)
 
 
-def pack_kernel(state_ref, far_ref, near_ref):
+def pack_kernel(state_ref, low_ref, high_ref, far_ref, near_ref):
     odd = lax.rem(lax.axis_index("grp"), 2) == 1
-    lanes = lane_index(ROWS)
-    left = jnp.zeros((ROWS, LANES), jnp.float32)
-    right = jnp.zeros((ROWS, LANES), jnp.float32)
-    for plane in range(PLANES):
-        tile = state_ref[plane]
-        keep = lanes >= HALO * plane
-        left = jnp.where(keep, pltpu.roll(tile, HALO * plane, 1) if plane else tile, left)
-        right = jnp.where(keep, pltpu.roll(tile, HALO * plane + HALO, 1), right)
-    far_ref[...] = jnp.where(odd, right, left)
-    near_ref[...] = jnp.where(odd, left, right)
+    for source, rows, start in ((low_ref, BAND, 0), (state_ref, ROWS, BAND), (high_ref, BAND, BAND + ROWS)):
+        lanes = lane_index(rows)
+        left = source[0]
+        right = pltpu.roll(source[0], HALO, 1)
+        for plane in range(1, PLANES):
+            keep = lanes >= HALO * plane
+            left = jnp.where(keep, pltpu.roll(source[plane], HALO * plane, 1), left)
+            right = jnp.where(keep, pltpu.roll(source[plane], HALO * plane + HALO, 1), right)
+        far_ref[start : start + rows] = jnp.where(odd, right, left)
+        near_ref[start : start + rows] = jnp.where(odd, left, right)
 
 
 def regroup(chunks):
@@ -75,7 +76,7 @@
 
 
 def rk_kernel(
-    coupling_ref, state_ref, low_ref, high_ref, far_ref, near_ref, under_ref, over_ref, heat_ref,
+    coupling_ref, state_ref, low_ref, high_ref, far_ref, near_ref, heat_ref,
     out_ref, send_ref, sa, sb, ta, tb, ua, ub, turn_sc,
 ):
     odd = lax.rem(lax.axis_index("grp"), 2) == 1
@@ -84,12 +85,9 @@
     has_high = lat < lax.axis_size("lat") - 1
     base = 16
 
-    far = jnp.concatenate([under_ref[0:BAND], far_ref[...], over_ref[0:BAND]], 0)
-    near = jnp.concatenate([under_ref[BAND:], near_ref[...], over_ref[BAND:]], 0)
-    left = jnp.where(odd, near, far)
-    right = jnp.where(odd, far, near)
-    span = ROWS + 2 * BAND
-    lanes = lane_index(span)
+    left = jnp.where(odd, near_ref[...], far_ref[...])
+    right = jnp.where(odd, far_ref[...], near_ref[...])
+    lanes = lane_index(SPAN)
     for plane in range(PLANES):
         sa[plane, base - BAND : base, :] = low_ref[plane]
         sa[plane, base : base + ROWS, :] = state_ref[plane]
@@ -218,6 +216,7 @@
 
 VMEM = pl.BlockSpec(memory_space=pltpu.VMEM)
 SMEM = pl.BlockSpec(memory_space=pltpu.SMEM)
+PARAMS = pltpu.CompilerParams(vmem_limit_bytes=16 * 1024 * 1024)
 
 
 def shape(*dims):
@@ -232,20 +231,19 @@
     planes = state.reshape(PLANES, ROWS, LANES)
     q = tracers.reshape(SPECIES, 128, 128)
 
+    count = lax.axis_size("lat")
+    low = lax.ppermute(planes[:, ROWS - BAND :], "lat", [(i, i + 1) for i in range(count - 1)])
+    high = lax.ppermute(planes[:, :BAND], "lat", [(i + 1, i) for i in range(count - 1)])
     far, near = pl.pallas_call(
         pack_kernel,
-        out_shape=(shape(ROWS, LANES), shape(ROWS, LANES)),
-        in_specs=[VMEM],
+        out_shape=(shape(SPAN, LANES), shape(SPAN, LANES)),
+        in_specs=[VMEM] * 3,
         out_specs=(VMEM, VMEM),
         cost_estimate=cost(1000000, 400000),
-    )(planes)
+        compiler_params=PARAMS,
+    )(planes, low, high)
     far_in = lax.ppermute(far, "grp", [(0, 3), (3, 0), (1, 2), (2, 1)])
     near_in = lax.ppermute(near, "grp", [(0, 1), (1, 0), (2, 3), (3, 2)])
-    count = lax.axis_size("lat")
-    up = [(i, i + 1) for i in range(count - 1)]
-    down = [(i + 1, i) for i in range(count - 1)]
-    low = lax.ppermute(planes[:, ROWS - BAND :], "lat", up)
-    high = lax.ppermute(planes[:, :BAND], "lat", down)
 
     pre, heat = pl.pallas_call(
         chem_kernel,
@@ -254,20 +252,19 @@
         out_specs=(VMEM, VMEM),
         scratch_shapes=[pltpu.VMEM((128, 128), jnp.float32), pltpu.VMEM((128, 128), jnp.float32)],
         cost_estimate=cost(10000000, 2000000),
+        compiler_params=PARAMS,
     )(rates, pairs, heat_map, heat_coef, q)
-
-    under = lax.ppermute(jnp.concatenate([far_in[ROWS - BAND :], near_in[ROWS - BAND :]], 0), "lat", up)
-    over = lax.ppermute(jnp.concatenate([far_in[:BAND], near_in[:BAND]], 0), "lat", down)
 
     extended = pltpu.VMEM((PLANES, 64, LANES), jnp.float32)
     stepped, send = pl.pallas_call(
         rk_kernel,
         out_shape=(shape(PLANES, ROWS, LANES), shape(PEERS * SLOTS, LANES)),
-        in_specs=[SMEM] + [VMEM] * 8,
+        in_specs=[SMEM] + [VMEM] * 6,
         out_specs=(VMEM, VMEM),
         scratch_shapes=[extended] * 6 + [pltpu.VMEM((3, 128, 128), jnp.float32)],
         cost_estimate=cost(20000000, 1500000),
-    )(coupling, planes, low, high, far_in, near_in, under, over, heat)
+        compiler_params=PARAMS,
+    )(coupling, planes, low, high, far_in, near_in, heat)
 
     received = lax.all_to_all(
         send.reshape(PEERS, SLOTS, LANES), "lon", split_axis=0, concat_axis=0, tiled=True
@@ -283,6 +280,7 @@
         scratch_shapes=[pltpu.VMEM((128, 128), jnp.float32), pltpu.VMEM((3, 128, 128), jnp.float32)],
         input_output_aliases={1: 0},
         cost_estimate=cost(10000000, 2500000),
+        compiler_params=PARAMS,
     )(received.reshape(PEERS * SLOTS, LANES), stepped.reshape(FIELDS, 128, 128), q, pre)
     return state_out.reshape(state.shape), q_out.reshape(tracers.shape)
 

time: 71.7 us -> 65.8 us (0.918)
  starting transfers between devices: 32.1 us -> 24.9 us
  waiting for transfers between devices: 0.14 us -> 7.12 us
  Pallas kernels: 14 us -> 9.88 us
  blocking collectives: 22.2 us -> 20.1 us
  local copies, waits for them, and re-layouts: 1.96 us -> 2.77 us
    ppermute x1, starting transfers between devices: 17.9 us -> 4.75 us  [on_device(): far_in = lax.ppermute(far, 'grp', [(0, 3), (3, 0), (1, 2), (2, 1)])]
    ppermute x4 -> x2, starting transfers between devices: 11.7 us -> 16.1 us  [the longest x1 14.2 us: on_device(): lax.ppermute(planes[:, :BAND], 'lat', [(i + 1, i) for i in range(count -...]
    ppermute x4 -> x2, waiting for transfers between devices: 0.14 us -> 4.41 us  [the longest x1 4.3 us: on_device(): lax.ppermute(planes[:, ROWS - BAND:], 'lat', [(i, i + 1) for i in range(c...]
    ppermute x1, waiting for transfers between devices: 0.01 us -> 2.71 us  [on_device(): far_in = lax.ppermute(far, 'grp', [(0, 3), (3, 0), (1, 2), (2, 1)])]
    all_to_all x1, blocking collectives: 22.2 us -> 20.1 us  [on_device(): lax.all_to_all(send.reshape(PEERS, SLOTS, LANES), 'lon', split_axis=0, co...]
    pallas_call x1, Pallas kernels: 1.88 us -> 0.31 us  [on_device(): pl.pallas_call(pack_kernel, out_shape=(shape(SPAN, LANES), shape(SPAN, LA...]
    ppermute x1, starting transfers between devices: 2.58 us -> 4.01 us  [on_device(): near_in = lax.ppermute(near, 'grp', [(0, 1), (1, 0), (2, 3), (3, 2)])]
    pallas_call x1, Pallas kernels: 2.92 us -> 1.84 us  [on_device(): pl.pallas_call(chem_kernel, out_shape=(shape(SPECIES, 128, 128), shape(4,...]
  transfers between devices with their start and end apart: 6 -> 4, of which waited for: 1 -> 3; matrix products, arithmetic and copies ran while one was open for 1% -> 0% of each run, Pallas kernels for 4% -> 3%
where the time goes in v2:
time: 65.8 us; the launch traced here: 65.4 us
  starting transfers between devices  24.9 us (38%)
  blocking collectives  20.1 us (31%)
  Pallas kernels  9.88 us (15%)
  waiting for transfers between devices  7.12 us (11%)
  local copies, waits for them, and re-layouts  2.77 us (4%)
  between operations  0.72 us (1%)
    all_to_all x1, blocking collectives, on_device(): lax.all_to_all(send.reshape(PEERS, SLOTS, LANES), 'lon', split_axis=0, co...  20.1 us
    ppermute x1, starting transfers between devices, on_device(): lax.ppermute(planes[:, :BAND], 'lat', [(i + 1, i) for i in range(count -...  14.2 us
    pallas_call x1, Pallas kernels, on_device(): pl.pallas_call(rk_kernel, out_shape=(shape(PLANES, ROWS, LANES), shape(PE...  5.3 us
    ppermute x1, starting transfers between devices, on_device(): far_in = lax.ppermute(far, 'grp', [(0, 3), (3, 0), (1, 2), (2, 1)])  4.75 us
    ppermute x1, waiting for transfers between devices, on_device(): lax.ppermute(planes[:, ROWS - BAND:], 'lat', [(i, i + 1) for i in range(c...  4.3 us
    ppermute x1, starting transfers between devices, on_device(): near_in = lax.ppermute(near, 'grp', [(0, 1), (1, 0), (2, 3), (3, 2)])  4.01 us
    ppermute x1, waiting for transfers between devices, on_device(): far_in = lax.ppermute(far, 'grp', [(0, 3), (3, 0), (1, 2), (2, 1)])  2.71 us
    pallas_call x1, Pallas kernels, on_device(): pl.pallas_call(final_kernel, grid=(1,), out_shape=(shape(FIELDS, 128, 128...  2.44 us
  transfers between devices with their start and end apart: 4, of which 3 were waited for; matrix products, arithmetic and copies ran while one was open for 0% of the time, Pallas kernels for 3%

profile of v2, /device:TPU:64, one launch (start us, length us, event | category | flops | bytes accessed | tf_op | source)
XLA Modules:
  0.0 65.4 jit_solution(11517108872525981150)
XLA Ops:
  0.6 0.0 copy-start
  0.6 1.0 %fusion = (f32[20,8,128]{2,1,0:T(8,128)S(1)}, f32[20,8,128]{2,1,0:T(8,128)S(1)}) fusion(f32[20,32,128]{2,1,0:T(8,128)} %bitcast.9), kind=kLoop, calls=%fused_computation | loop fusion | bytes 327680 | tf_op jit(solution)/shard_map/slice | solution.py:236
  1.7 14.2 %collective-permute-start.1 = (f32[20,8,128]{2,1,0:T(8,128)S(1)}, f32[20,8,128]{2,1,0:T(8,128)S(1)}, u32[]{:S(2)}, u32[]{:S(2)}) collective-permute-start(f32[20,8,128]{2,1,0:T(8,128)S(1)} %get-tuple-element.18), channel_id=1, source_target_pairs={{32,0},{64,32},{96,64},{128,96},{160,128},{192,160},{224,192},{33,... | collective-permute-start | bytes 245768 | tf_op jit(solution)/shard_map/ppermute | solution.py:236
  15.8 1.9 %collective-permute-start = (f32[20,8,128]{2,1,0:T(8,128)S(1)}, f32[20,8,128]{2,1,0:T(8,128)S(1)}, u32[]{:S(2)}, u32[]{:S(2)}) collective-permute-start(f32[20,8,128]{2,1,0:T(8,128)S(1)} %get-tuple-element.19), channel_id=1, source_target_pairs={{0,32},{32,64},{64,96},{96,128},{128,160},{160,192},{192,224},{1,3... | collective-permute-start | bytes 245768 | tf_op jit(solution)/shard_map/ppermute | solution.py:235
  17.8 0.1 collective-permute-done.1.high_ref
  17.9 4.3 %collective-permute-done.low_ref = f32[20,8,128]{2,1,0:T(8,128)S(1)} collective-permute-done((f32[20,8,128]{2,1,0:T(8,128)S(1)}, f32[20,8,128]{2,1,0:T(8,128)S(1)}, u32[]{:S(2)}, u32[]{:S(2)}) %collective-permute-start) | collective-permute-done | bytes 81952 | tf_op jit(solution)/shard_map/ppermute | solution.py:235
  22.2 0.0 copy-start.1
  22.2 1.0 %copy-done.1 = f32[5,4,32,128]{3,2,1,0:T(8,128)S(1)} copy-done((f32[5,4,32,128]{3,2,1,0:T(8,128)S(1)}, f32[5,4,32,128]{3,2,1,0:T(8,128)}, u32[]{:S(2)}) %copy-start.1) | copy-done | bytes 327704
  23.2 0.3 shard_map.86
  23.5 0.0 copy-start.7
  23.5 4.7 %collective-permute-start.2 = (f32[48,128]{1,0:T(8,128)S(1)}, f32[48,128]{1,0:T(8,128)S(1)}, u32[]{:S(2)}, u32[]{:S(2)}) collective-permute-start(f32[48,128]{1,0:T(8,128)S(1)} %get-tuple-element.10), channel_id=1, source_target_pairs={{0,768},{768,0},{256,512},{512,256},{1,769},{769,1},{257,513},{513... | collective-permute-start | bytes 73736 | tf_op jit(solution)/shard_map/ppermute | solution.py:245
  28.2 4.0 %collective-permute-start.3 = (f32[48,128]{1,0:T(8,128)S(1)}, f32[48,128]{1,0:T(8,128)S(1)}, u32[]{:S(2)}, u32[]{:S(2)}) collective-permute-start(f32[48,128]{1,0:T(8,128)S(1)} %get-tuple-element.11), channel_id=1, source_target_pairs={{0,256},{256,0},{512,768},{768,512},{1,257},{257,1},{513,769},{769... | collective-permute-start | bytes 73736 | tf_op jit(solution)/shard_map/ppermute | solution.py:246
  32.3 0.0 copy-done.7
  32.3 0.1 copy.10.pairs_ref
  32.4 0.0 copy-start.4
  32.4 0.0 copy-start.5
  32.4 0.0 copy-start.6
  32.4 0.0 copy-done
  32.4 0.6 copy-done.4
  33.0 0.0 copy-done.5
  33.0 0.0 copy-done.6
  33.0 0.0 copy-start.2
  33.0 0.0 copy-start.3
  33.0 1.8 %shard_map.87 = (f32[12,128,128]{2,1,0:T(8,128)S(1)}, f32[4,32,128]{2,1,0:T(8,128)S(1)}) custom-call(f32[24]{0:T(128)S(1)} %copy-done.4, s32[24,3]{1,0:T(8,128)S(1)} %copy.10.pairs_ref, s32[12]{0:T(128)S(1)} %copy-done.5, f32[4]{0:T(128)S(1)} %copy-done.6, f32[12,128,128]{2,1,0:T(8,128)S(1)} %bitcast.7), custom_call_target="tpu_custom_call" | custom-call | flops 10000000 | bytes 2000000 | tf_op jit(solution)/shard_map/pallas_call | solution.py:248
  34.9 2.7 %collective-permute-done.2.far_ref = f32[48,128]{1,0:T(8,128)S(1)} collective-permute-done((f32[48,128]{1,0:T(8,128)S(1)}, f32[48,128]{1,0:T(8,128)S(1)}, u32[]{:S(2)}, u32[]{:S(2)}) %collective-permute-start.2) | collective-permute-done | bytes 24608 | tf_op jit(solution)/shard_map/ppermute | solution.py:245
  37.6 0.0 collective-permute-done.3.near_ref
  37.6 0.0 copy-done.2
  37.6 0.0 copy-done.3
  37.6 5.3 %shard_map.88 = (f32[20,32,128]{2,1,0:T(8,128)}, f32[512,128]{1,0:T(8,128)S(1)}) custom-call(f32[5,5]{1,0:T(8,128)S(1)} %copy-done.3, f32[20,32,128]{2,1,0:T(8,128)S(1)} %bitcast.11, f32[20,8,128]{2,1,0:T(8,128)S(1)} %collective-permute-done.low_ref, f32[20,8,128]{2,1,0:T(8,128)S(1)} %collective-permute-done.1.high_ref, ...), custom_call_target="tpu_custom_call" | custom-call | flops 20000000 | bytes 1500000 | tf_op jit(solution)/shard_map/pallas_call | solution.py:259
  42.9 20.1 %all_to_all.5 = f32[32,16,128]{2,1,0:T(8,128)S(1)} all-to-all(f32[32,16,128]{2,1,0:T(8,128)S(1)} %bitcast.13), channel_id=1, replica_groups=mesh['grp'=4,'lat'=8,'lon'=32] {'lon'}, dimensions={0} | all-to-all | bytes 524288 | tf_op jit(solution)/shard_map/all_to_all | solution.py:269
  63.0 2.4 %shard_map.89 = (f32[5,128,128]{2,1,0:T(8,128)}, f32[12,128,128]{2,1,0:T(8,128)}) custom-call(f32[512,128]{1,0:T(8,128)S(1)} %bitcast.12, f32[5,128,128]{2,1,0:T(8,128)} %bitcast.14, f32[12,128,128]{2,1,0:T(8,128)S(1)} %bitcast.8, f32[12,128,128]{2,1,0:T(8,128)S(1)} %get-tuple-element.15.pre_ref), custom_call_target="tpu_custom_call", output_to_operand_aliasing={{0}: (1, {})} | custom-call | flops 10000000 | bytes 2500000 | tf_op jit(solution)/shard_map/pallas_call | solution.py:274
Async XLA Ops:
  0.6 31.7 %copy-start = (f32[12,32,4,128]{3,2,1,0:T(4,128)S(1)}, f32[12,32,4,128]{3,2,1,0:T(4,128)}, u32[]{:S(2)}) copy-start(f32[12,32,4,128]{3,2,1,0:T(4,128)} %param.8) | copy-start | bytes 2359300
  1.7 16.2 %collective-permute-start.1 = (f32[20,8,128]{2,1,0:T(8,128)S(1)}, f32[20,8,128]{2,1,0:T(8,128)S(1)}, u32[]{:S(2)}, u32[]{:S(2)}) collective-permute-start(f32[20,8,128]{2,1,0:T(8,128)S(1)} %get-tuple-element.18), channel_id=1, source_target_pairs={{32,0},{64,32},{96,64},{128,96},{160,128},{192,160},{224,192},{33,... | collective-permute-start | bytes 245768 | tf_op jit(solution)/shard_map/ppermute | solution.py:236
  15.8 6.3 %collective-permute-start = (f32[20,8,128]{2,1,0:T(8,128)S(1)}, f32[20,8,128]{2,1,0:T(8,128)S(1)}, u32[]{:S(2)}, u32[]{:S(2)}) collective-permute-start(f32[20,8,128]{2,1,0:T(8,128)S(1)} %get-tuple-element.19), channel_id=1, source_target_pairs={{0,32},{32,64},{64,96},{96,128},{128,160},{160,192},{192,224},{1,3... | collective-permute-start | bytes 245768 | tf_op jit(solution)/shard_map/ppermute | solution.py:235
  22.2 1.0 %copy-start.1 = (f32[5,4,32,128]{3,2,1,0:T(8,128)S(1)}, f32[5,4,32,128]{3,2,1,0:T(8,128)}, u32[]{:S(2)}) copy-start(f32[5,4,32,128]{3,2,1,0:T(8,128)} %param.7) | copy-start | bytes 983044
  23.5 8.8 %copy-start.7 = (s32[24,3]{0,1:T(4,128)S(1)}, s32[24,3]{0,1:T(4,128)}, u32[]{:S(2)}) copy-start(s32[24,3]{0,1:T(4,128)} %param.11) | copy-start | bytes 868
  23.5 14.1 %collective-permute-start.2 = (f32[48,128]{1,0:T(8,128)S(1)}, f32[48,128]{1,0:T(8,128)S(1)}, u32[]{:S(2)}, u32[]{:S(2)}) collective-permute-start(f32[48,128]{1,0:T(8,128)S(1)} %get-tuple-element.10), channel_id=1, source_target_pairs={{0,768},{768,0},{256,512},{512,256},{1,769},{769,1},{257,513},{513... | collective-permute-start | bytes 73736 | tf_op jit(solution)/shard_map/ppermute | solution.py:245
  28.2 9.4 %collective-permute-start.3 = (f32[48,128]{1,0:T(8,128)S(1)}, f32[48,128]{1,0:T(8,128)S(1)}, u32[]{:S(2)}, u32[]{:S(2)}) collective-permute-start(f32[48,128]{1,0:T(8,128)S(1)} %get-tuple-element.11), channel_id=1, source_target_pairs={{0,256},{256,0},{512,768},{768,512},{1,257},{257,1},{513,769},{769... | collective-permute-start | bytes 73736 | tf_op jit(solution)/shard_map/ppermute | solution.py:246
  32.4 0.7 %copy-start.4 = (f32[24]{0:T(128)S(1)}, f32[24]{0:T(128)}, u32[]{:S(2)}) copy-start(f32[24]{0:T(128)} %rates_ref.1) | copy-start | bytes 292
  32.4 0.7 %copy-start.5 = (s32[12]{0:T(128)S(1)}, s32[12]{0:T(128)}, u32[]{:S(2)}) copy-start(s32[12]{0:T(128)} %map_ref.1) | copy-start | bytes 148
  32.4 0.7 %copy-start.6 = (f32[4]{0:T(128)S(1)}, f32[4]{0:T(128)}, u32[]{:S(2)}) copy-start(f32[4]{0:T(128)} %coef_ref.1) | copy-start | bytes 52
  33.0 4.6 %copy-start.2 = (f32[5,4,32,128]{3,2,1,0:T(8,128)S(1)}, f32[5,4,32,128]{3,2,1,0:T(8,128)}, u32[]{:S(2)}) copy-start(f32[5,4,32,128]{3,2,1,0:T(8,128)} %param.7) | copy-start | bytes 983044
  33.0 4.6 %copy-start.3 = (f32[5,5]{1,0:T(8,128)S(1)}, f32[5,5]{1,0:T(8,128)}, u32[]{:S(2)}) copy-start(f32[5,5]{1,0:T(8,128)} %coupling_ref.1) | copy-start | bytes 304

commit v3 on v2

--- a/solution.py
+++ b/solution.py
@@ -1,3 +1,5 @@
+import functools
+
 import jax
 import jax.numpy as jnp
 from jax import lax
@@ -23,18 +25,29 @@
     return lax.broadcasted_iota(jnp.int32, (rows, LANES), 1)
 
 
-def pack_kernel(state_ref, low_ref, high_ref, far_ref, near_ref):
+def packed(source):
+    lanes = lane_index(source.shape[1])
+    left = source[0]
+    right = pltpu.roll(source[0], HALO, 1)
+    for plane in range(1, PLANES):
+        keep = lanes >= HALO * plane
+        left = jnp.where(keep, pltpu.roll(source[plane], HALO * plane, 1), left)
+        right = jnp.where(keep, pltpu.roll(source[plane], HALO * plane + HALO, 1), right)
     odd = lax.rem(lax.axis_index("grp"), 2) == 1
-    for source, rows, start in ((low_ref, BAND, 0), (state_ref, ROWS, BAND), (high_ref, BAND, BAND + ROWS)):
-        lanes = lane_index(rows)
-        left = source[0]
-        right = pltpu.roll(source[0], HALO, 1)
-        for plane in range(1, PLANES):
-            keep = lanes >= HALO * plane
-            left = jnp.where(keep, pltpu.roll(source[plane], HALO * plane, 1), left)
-            right = jnp.where(keep, pltpu.roll(source[plane], HALO * plane + HALO, 1), right)
-        far_ref[start : start + rows] = jnp.where(odd, right, left)
-        near_ref[start : start + rows] = jnp.where(odd, left, right)
+    return jnp.where(odd, right, left), jnp.where(odd, left, right)
+
+
+def edge_kernel(state_ref, top_ref, bottom_ref, far_ref, near_ref):
+    top_ref[...] = state_ref[:, :BAND]
+    bottom_ref[...] = state_ref[:, ROWS - BAND :]
+    far_ref[...], near_ref[...] = packed(state_ref)
+
+
+def pack_kernel(low_ref, high_ref, own_far_ref, own_near_ref, far_ref, near_ref):
+    far_ref[BAND : BAND + ROWS] = own_far_ref[...]
+    near_ref[BAND : BAND + ROWS] = own_near_ref[...]
+    far_ref[:BAND], near_ref[:BAND] = packed(low_ref)
+    far_ref[BAND + ROWS :], near_ref[BAND + ROWS :] = packed(high_ref)
 
 
 def regroup(chunks):
@@ -51,7 +64,27 @@
     return out
 
 
-def chem_kernel(rates_ref, pairs_ref, map_ref, coef_ref, q_ref, pre_ref, heat_ref, heat_sc, turn_sc):
+def runs_here(early):
+    first = lax.axis_index("grp") < lax.axis_size("grp") // 2
+    return first if early else jnp.logical_not(first)
+
+
+def chem_kernel(early, rates_ref, pairs_ref, map_ref, coef_ref, q_ref, *refs):
+    pre_ref, heat_ref, heat_sc, turn_sc = refs[-4:]
+
+    @pl.when(runs_here(early))
+    def _():
+        chemistry(rates_ref, pairs_ref, map_ref, coef_ref, q_ref, pre_ref, heat_ref, heat_sc, turn_sc)
+
+    if not early:
+
+        @pl.when(runs_here(True))
+        def _():
+            pre_ref[...] = refs[0][...]
+            heat_ref[...] = refs[1][...]
+
+
+def chemistry(rates_ref, pairs_ref, map_ref, coef_ref, q_ref, pre_ref, heat_ref, heat_sc, turn_sc):
     pre_ref[...] = q_ref[...]
     heat_sc[...] = jnp.zeros_like(heat_sc)
 
@@ -59,7 +92,7 @@
         return coef_ref[map_ref[species]]
 
     def react(r, carry):
-        a, b, p = pairs_ref[r, 0], pairs_ref[r, 1], pairs_ref[r, 2]
+        a, b, p = pairs_ref[0, r], pairs_ref[1, r], pairs_ref[2, r]
         rate = rates_ref[r] * q_ref[a] * q_ref[b]
         heat_sc[...] += (weight(p) - weight(a) - weight(b)) * rate
         pre_ref[p] += rate
@@ -75,27 +108,34 @@
         heat_ref[y] = block
 
 
-def rk_kernel(
-    coupling_ref, state_ref, low_ref, high_ref, far_ref, near_ref, heat_ref,
-    out_ref, send_ref, sa, sb, ta, tb, ua, ub, turn_sc,
-):
-    odd = lax.rem(lax.axis_index("grp"), 2) == 1
+def lat_ends():
     lat = lax.axis_index("lat")
-    has_low = lat > 0
-    has_high = lat < lax.axis_size("lat") - 1
+    return lat > 0, lat < lax.axis_size("lat") - 1
+
+
+def rk_kernel(early, coupling_ref, state_ref, low_ref, high_ref, *refs):
+    out_ref = refs[-7]
+
+    @pl.when(runs_here(early))
+    def _():
+        whole_step(coupling_ref, state_ref, low_ref, high_ref, *refs[-7:])
+
+    if not early:
+
+        @pl.when(runs_here(True))
+        def _():
+            out_ref[...] = refs[0][...]
+
+
+def whole_step(coupling_ref, state_ref, low_ref, high_ref, out_ref, sa, sb, ta, tb, ua, ub):
+    has_low, has_high = lat_ends()
     base = 16
 
-    left = jnp.where(odd, near_ref[...], far_ref[...])
-    right = jnp.where(odd, far_ref[...], near_ref[...])
-    lanes = lane_index(SPAN)
+    sb[...] = jnp.zeros_like(sb)
     for plane in range(PLANES):
         sa[plane, base - BAND : base, :] = low_ref[plane]
         sa[plane, base : base + ROWS, :] = state_ref[plane]
         sa[plane, base + ROWS : base + ROWS + BAND, :] = high_ref[plane]
-        beyond = pltpu.roll(right, (-HALO * plane) % LANES, 1) if plane else right
-        before = pltpu.roll(left, (LANES - HALO - HALO * plane) % LANES, 1)
-        edge = jnp.where(lanes >= LANES - HALO, before, 0.0)
-        sb[plane, base - BAND : base + ROWS + BAND, :] = jnp.where(lanes < HALO, beyond, edge)
 
     lane8 = lane_index(8)
     weights = [
@@ -166,6 +206,78 @@
     lax.fori_loop(0, LEVELS, stage_one, 0)
     lax.fori_loop(0, LEVELS, stage_two, 0)
     lax.fori_loop(0, LEVELS, stage_three, 0)
+
+
+def edge_step_kernel(
+    coupling_ref, main_ref, far_ref, near_ref, heat_ref, out_ref, send_ref, sa, sb, ta, tb, ua, ub, turn_sc
+):
+    odd = lax.rem(lax.axis_index("grp"), 2) == 1
+    has_low, has_high = lat_ends()
+    pad = 8
+    zero = jnp.zeros((SPAN, LANES), jnp.float32)
+    sa[pad : pad + SPAN, :] = jnp.where(odd, near_ref[...], far_ref[...])
+    sa[pad + SPAN : pad + 2 * SPAN, :] = zero
+    sb[pad : pad + SPAN, :] = zero
+    sb[pad + SPAN : pad + 2 * SPAN, :] = jnp.where(odd, far_ref[...], near_ref[...])
+
+    lanes = lane_index(8)
+    column = lax.rem(lanes, HALO)
+    field = lanes // (HALO * LEVELS)
+    mixes = {}
+    for d in range(1 - FIELDS, FIELDS):
+        total = jnp.zeros((8, LANES), jnp.float32)
+        for f in range(max(d, 0), min(FIELDS, FIELDS + d)):
+            total = jnp.where(field == f, coupling_ref[f, f - d] + (0.6 if d == 0 else 0.0), total)
+        mixes[d] = total
+
+    def turn(value, by):
+        return pltpu.roll(value, by % LANES, 1) if by % LANES else value
+
+    def apply(a_ref, b_ref, row):
+        a, b = a_ref[row : row + 8, :], b_ref[row : row + 8, :]
+        ya, yb = {}, {}
+        for j in (1, 2):
+            inside, behind = column < HALO - j, column >= j
+            ya[j] = jnp.where(inside, turn(a, -j), turn(b, HALO - j))
+            yb[j] = jnp.where(inside, turn(b, -j), 0.0)
+            ya[-j] = jnp.where(behind, turn(a, j), 0.0)
+            yb[-j] = jnp.where(behind, turn(b, j), turn(a, j - HALO))
+        out = []
+        for value, ref, y in ((a, a_ref, ya), (b, b_ref, yb)):
+            x = {j: ref[row + j : row + j + 8, :] for j in (1, 2, -1, -2)}
+            total = -0.1 * (x[1] + y[1]) + 0.3 * (x[-1] + y[-1])
+            total = total + 0.025 * ((x[2] - x[-2]) + (y[2] - y[-2]))
+            for d, mix in mixes.items():
+                total = total + mix * turn(value, HALO * LEVELS * d)
+            out.append(total)
+        return out
+
+    def masked(value, row):
+        place = (row - pad) % SPAN
+        if place < BAND:
+            return jnp.where(has_low, value, 0.0)
+        if place >= BAND + ROWS:
+            return jnp.where(has_high, value, 0.0)
+        return value
+
+    every = range(pad, pad + 2 * SPAN, 8)
+    for row in every:
+        a, b = apply(sa, sb, row)
+        ta[row : row + 8, :] = masked(a, row)
+        tb[row : row + 8, :] = masked(b, row)
+    for row in every:
+        a, b = apply(ta, tb, row)
+        ua[row : row + 8, :] = masked(0.75 * sa[row : row + 8, :] + 0.25 * a, row)
+        ub[row : row + 8, :] = masked(0.75 * sb[row : row + 8, :] + 0.25 * b, row)
+    for row in range(pad + BAND, pad + BAND + ROWS, 8):
+        _, b = apply(ua, ub, row)
+        a, _ = apply(ua, ub, row + SPAN)
+        first, final = (2.0 / 3.0) * b, (2.0 / 3.0) * a
+        place = row - pad - BAND
+        for plane in range(PLANES):
+            gain = jnp.where(lanes < HALO, turn(first, -HALO * plane), 0.0)
+            gain = jnp.where(lanes >= LANES - HALO, turn(final, LANES - HALO - HALO * plane), gain)
+            out_ref[plane, place : place + 8, :] = main_ref[plane, place : place + 8, :] + gain
 
     for f in range(3):
         plane = jnp.concatenate([out_ref[f * LEVELS + z] for z in range(LEVELS)], 0)
@@ -231,40 +343,72 @@
     planes = state.reshape(PLANES, ROWS, LANES)
     q = tracers.reshape(SPECIES, 128, 128)
 
+    top, bottom, own_far, own_near = pl.pallas_call(
+        edge_kernel,
+        out_shape=(shape(PLANES, BAND, LANES),) * 2 + (shape(ROWS, LANES),) * 2,
+        in_specs=[VMEM],
+        out_specs=(VMEM,) * 4,
+        cost_estimate=cost(1000000, 500000),
+        compiler_params=PARAMS,
+    )(planes)
     count = lax.axis_size("lat")
-    low = lax.ppermute(planes[:, ROWS - BAND :], "lat", [(i, i + 1) for i in range(count - 1)])
-    high = lax.ppermute(planes[:, :BAND], "lat", [(i + 1, i) for i in range(count - 1)])
+    low = lax.ppermute(bottom, "lat", [(i, i + 1) for i in range(count - 1)])
+    high = lax.ppermute(top, "lat", [(i + 1, i) for i in range(count - 1)])
+    reactants = (rates, pairs.T, heat_map, heat_coef, q)
+
+    def chem(early, *before):
+        return pl.pallas_call(
+            functools.partial(chem_kernel, early),
+            out_shape=(shape(SPECIES, 128, 128), shape(4, PEERS, LANES)),
+            in_specs=[SMEM, SMEM, SMEM, SMEM, VMEM] + [VMEM] * len(before),
+            out_specs=(VMEM, VMEM),
+            scratch_shapes=[pltpu.VMEM((128, 128), jnp.float32), pltpu.VMEM((128, 128), jnp.float32)],
+            input_output_aliases={5 + i: i for i in range(len(before))},
+            cost_estimate=cost(10000000, 2000000),
+            compiler_params=PARAMS,
+        )(*reactants, *before)
+
+    extended = pltpu.VMEM((PLANES, 64, LANES), jnp.float32)
+
+    def rk(early, *before):
+        return pl.pallas_call(
+            functools.partial(rk_kernel, early),
+            out_shape=shape(PLANES, ROWS, LANES),
+            in_specs=[SMEM] + [VMEM] * (3 + len(before)),
+            out_specs=VMEM,
+            scratch_shapes=[extended] * 6,
+            input_output_aliases={4 + i: i for i in range(len(before))},
+            cost_estimate=cost(20000000, 1500000),
+            compiler_params=PARAMS,
+        )(coupling, planes, low, high, *before)
+
+    pre, heat = chem(True)
+    low, high, heat = lax.optimization_barrier((low, high, heat))
+    main = rk(True)
+    low, high, main = lax.optimization_barrier((low, high, main))
     far, near = pl.pallas_call(
         pack_kernel,
         out_shape=(shape(SPAN, LANES), shape(SPAN, LANES)),
-        in_specs=[VMEM] * 3,
+        in_specs=[VMEM] * 4,
         out_specs=(VMEM, VMEM),
         cost_estimate=cost(1000000, 400000),
         compiler_params=PARAMS,
-    )(planes, low, high)
+    )(low, high, own_far, own_near)
+    far, near, low, high, main, pre, heat = lax.optimization_barrier((far, near, low, high, main, pre, heat))
     far_in = lax.ppermute(far, "grp", [(0, 3), (3, 0), (1, 2), (2, 1)])
     near_in = lax.ppermute(near, "grp", [(0, 1), (1, 0), (2, 3), (3, 2)])
-
-    pre, heat = pl.pallas_call(
-        chem_kernel,
-        out_shape=(shape(SPECIES, 128, 128), shape(4, PEERS, LANES)),
-        in_specs=[SMEM, SMEM, SMEM, SMEM, VMEM],
+    pre, heat = chem(False, pre, heat)
+    main = rk(False, main)
+    window = pltpu.VMEM((2 * SPAN + 16, LANES), jnp.float32)
+    stepped, send = pl.pallas_call(
+        edge_step_kernel,
+        out_shape=(shape(PLANES, ROWS, LANES), shape(PEERS * SLOTS, LANES)),
+        in_specs=[SMEM] + [VMEM] * 4,
         out_specs=(VMEM, VMEM),
-        scratch_shapes=[pltpu.VMEM((128, 128), jnp.float32), pltpu.VMEM((128, 128), jnp.float32)],
-        cost_estimate=cost(10000000, 2000000),
+        scratch_shapes=[window] * 6 + [pltpu.VMEM((3, 128, 128), jnp.float32)],
+        cost_estimate=cost(2000000, 1000000),
         compiler_params=PARAMS,
-    )(rates, pairs, heat_map, heat_coef, q)
-
-    extended = pltpu.VMEM((PLANES, 64, LANES), jnp.float32)
-    stepped, send = pl.pallas_call(
-        rk_kernel,
-        out_shape=(shape(PLANES, ROWS, LANES), shape(PEERS * SLOTS, LANES)),
-        in_specs=[SMEM] + [VMEM] * 6,
-        out_specs=(VMEM, VMEM),
-        scratch_shapes=[extended] * 6 + [pltpu.VMEM((3, 128, 128), jnp.float32)],
-        cost_estimate=cost(20000000, 1500000),
-        compiler_params=PARAMS,
-    )(coupling, planes, low, high, far_in, near_in, heat)
+    )(coupling, main, far_in, near_in, heat)
 
     received = lax.all_to_all(
         send.reshape(PEERS, SLOTS, LANES), "lon", split_axis=0, concat_axis=0, tiled=True

time: 65.8 us -> 63.1 us (0.959)
  the two profiles are of different devices: /device:TPU:64 before, /device:TPU:8 now
where the time goes in v3:
time: 63.1 us; the launch traced here: 62.7 us
  blocking collectives  22.3 us (35%)
  starting transfers between devices  22 us (35%)
  Pallas kernels  13 us (21%)
  local copies, waits for them, and re-layouts  2.77 us (4%)
  waiting for transfers between devices  1.87 us (3%)
  between operations  0.78 us (1%)
    all_to_all x1, blocking collectives, on_device(): lax.all_to_all(send.reshape(PEERS, SLOTS, LANES), 'lon', split_axis=0, co...  22.3 us
    ppermute x1, starting transfers between devices, on_device(): far_in = lax.ppermute(far, 'grp', [(0, 3), (3, 0), (1, 2), (2, 1)])  12.4 us
    pallas_call x2, Pallas kernels, rk(): pl.pallas_call(functools.partial(rk_kernel, early), out_shape=shape(PLANE...  5 us
    ppermute x1, starting transfers between devices, on_device(): low = lax.ppermute(bottom, 'lat', [(i, i + 1) for i in range(count - 1)])  4.28 us
    ppermute x1, starting transfers between devices, on_device(): near_in = lax.ppermute(near, 'grp', [(0, 1), (1, 0), (2, 3), (3, 2)])  4.01 us
    pallas_call x1, Pallas kernels, on_device(): pl.pallas_call(edge_step_kernel, out_shape=(shape(PLANES, ROWS, LANES), s...  2.77 us
    unnamed x18, local copies, waits for them, and re-layouts  2.77 us
    pallas_call x1, Pallas kernels, on_device(): pl.pallas_call(final_kernel, grid=(1,), out_shape=(shape(FIELDS, 128, 128...  2.43 us
  transfers between devices with their start and end apart: 4, of which 1 were waited for; matrix products, arithmetic and copies ran while one was open for 0% of the time, Pallas kernels for 5%

profile of v3, /device:TPU:8, one launch (start us, length us, event | category | flops | bytes accessed | tf_op | source)
XLA Modules:
  0.0 62.7 jit_solution(13935276747631911430)
XLA Ops:
  0.6 0.0 copy-start.2
  0.6 1.0 %copy-done.2 = f32[5,4,32,128]{3,2,1,0:T(8,128)S(1)} copy-done((f32[5,4,32,128]{3,2,1,0:T(8,128)S(1)}, f32[5,4,32,128]{3,2,1,0:T(8,128)}, u32[]{:S(2)}) %copy-start.2) | copy-done | bytes 327704
  1.6 0.0 copy-start.3
  1.6 0.2 shard_map.86
  1.8 4.3 %collective-permute-start = (f32[20,8,128]{2,1,0:T(8,128)S(1)}, f32[20,8,128]{2,1,0:T(8,128)S(1)}, u32[]{:S(2)}, u32[]{:S(2)}) collective-permute-start(f32[20,8,128]{2,1,0:T(8,128)S(1)} %get-tuple-element.29), channel_id=1, source_target_pairs={{0,32},{32,64},{64,96},{96,128},{128,160},{160,192},{192,224},{1,3... | collective-permute-start | bytes 245768 | tf_op jit(solution)/shard_map/ppermute | solution.py:355
  6.1 0.0 copy-start.5
  6.1 1.3 %collective-permute-start.1 = (f32[20,8,128]{2,1,0:T(8,128)S(1)}, f32[20,8,128]{2,1,0:T(8,128)S(1)}, u32[]{:S(2)}, u32[]{:S(2)}) collective-permute-start(f32[20,8,128]{2,1,0:T(8,128)S(1)} %get-tuple-element.30), channel_id=1, source_target_pairs={{32,0},{64,32},{96,64},{128,96},{160,128},{192,160},{224,192},{33,... | collective-permute-start | bytes 245768 | tf_op jit(solution)/shard_map/ppermute | solution.py:356
  7.4 0.0 copy-start.6
  7.4 0.0 copy-start.7
  7.5 0.0 copy-start.8
  7.5 0.0 copy-done.5
  7.5 0.6 copy-done.6
  8.1 0.0 copy-done.7
  8.1 0.0 copy-done.8
  8.1 0.0 copy-start
  8.1 1.1 %copy-done = f32[12,32,4,128]{3,2,1,0:T(4,128)S(1)} copy-done((f32[12,32,4,128]{3,2,1,0:T(4,128)S(1)}, f32[12,32,4,128]{3,2,1,0:T(4,128)}, u32[]{:S(2)}) %copy-start) | copy-done | bytes 786456
  9.3 0.0 copy-start.4
  9.3 0.0 copy-start.1
  9.3 1.7 %shard_map.87 = (f32[12,128,128]{2,1,0:T(8,128)S(1)}, f32[4,32,128]{2,1,0:T(8,128)S(1)}) custom-call(f32[24]{0:T(128)S(1)} %copy-done.6, s32[3,24]{1,0:T(4,128)S(1)} %bitcast.16, s32[12]{0:T(128)S(1)} %copy-done.7, f32[4]{0:T(128)S(1)} %copy-done.8, f32[12,128,128]{2,1,0:T(8,128)S(1)} %bitcast.8), custom_call_target="tpu_custom_call" | custom-call | flops 10000000 | bytes 2000000 | tf_op jit(solution)/shard_map/pallas_call | solution.py:360
  11.0 0.0 collective-permute-done.low_ref
  11.0 1.9 %collective-permute-done.1.high_ref = f32[20,8,128]{2,1,0:T(8,128)S(1)} collective-permute-done((f32[20,8,128]{2,1,0:T(8,128)S(1)}, f32[20,8,128]{2,1,0:T(8,128)S(1)}, u32[]{:S(2)}, u32[]{:S(2)}) %collective-permute-start.1) | collective-permute-done | bytes 81952 | tf_op jit(solution)/shard_map/ppermute | solution.py:356
  12.8 0.0 copy-done.3
  12.8 0.0 copy-done.4
  12.8 4.3 %shard_map.88.refs_0_ = f32[20,32,128]{2,1,0:T(8,128)S(1)} custom-call(f32[5,5]{1,0:T(8,128)S(1)} %copy-done.4, f32[20,32,128]{2,1,0:T(8,128)S(1)} %bitcast.12, f32[20,8,128]{2,1,0:T(8,128)S(1)} %collective-permute-done.low_ref, f32[20,8,128]{2,1,0:T(8,128)S(1)} %collective-permute-done.1.high_ref), custom_call_target="tpu_custom_call" | custom-call | flops 20000000 | bytes 1500000 | tf_op jit(solution)/shard_map/pallas_call | solution.py:374
  17.2 0.1 shard_map.89
  17.3 12.4 %collective-permute-start.2 = (f32[48,128]{1,0:T(8,128)S(1)}, f32[48,128]{1,0:T(8,128)S(1)}, u32[]{:S(2)}, u32[]{:S(2)}) collective-permute-start(f32[48,128]{1,0:T(8,128)S(1)} %get-tuple-element.46), channel_id=1, source_target_pairs={{0,768},{768,0},{256,512},{512,256},{1,769},{769,1},{257,513},{513... | collective-permute-start | bytes 73736 | tf_op jit(solution)/shard_map/ppermute | solution.py:398
  29.7 4.0 %collective-permute-start.3 = (f32[48,128]{1,0:T(8,128)S(1)}, f32[48,128]{1,0:T(8,128)S(1)}, u32[]{:S(2)}, u32[]{:S(2)}) collective-permute-start(f32[48,128]{1,0:T(8,128)S(1)} %get-tuple-element.47), channel_id=1, source_target_pairs={{0,256},{256,0},{512,768},{768,512},{1,257},{257,1},{513,769},{769... | collective-permute-start | bytes 73736 | tf_op jit(solution)/shard_map/ppermute | solution.py:399
  33.8 0.0 copy-done.1
  33.8 0.7 %shard_map.91 = (f32[12,128,128]{2,1,0:T(8,128)S(1)}, f32[4,32,128]{2,1,0:T(8,128)S(1)}) custom-call(f32[24]{0:T(128)S(1)} %copy-done.6, s32[3,24]{1,0:T(4,128)S(1)} %bitcast.17, s32[12]{0:T(128)S(1)} %copy-done.7, f32[4]{0:T(128)S(1)} %copy-done.8, f32[12,128,128]{2,1,0:T(8,128)S(1)} %bitcast.9, ...), custom_call_target="tpu_custom_call", output_to_operand_aliasing={{0}: (5, {}), {1}: (6, {})} | custom-call | flops 10000000 | bytes 2000000 | tf_op jit(solution)/shard_map/pallas_call | solution.py:360
  34.5 0.7 %shard_map.90.main_ref = f32[20,32,128]{2,1,0:T(8,128)S(1)} custom-call(f32[5,5]{1,0:T(8,128)S(1)} %copy-done.4, f32[20,32,128]{2,1,0:T(8,128)S(1)} %bitcast.13, f32[20,8,128]{2,1,0:T(8,128)S(1)} %collective-permute-done.low_ref, f32[20,8,128]{2,1,0:T(8,128)S(1)} %collective-permute-done.1.high_ref, ...), custom_call_target="tpu_custom_call", output_to_operand_aliasing={{}: (4, {})} | custom-call | flops 20000000 | bytes 1500000 | tf_op jit(solution)/shard_map/pallas_call | solution.py:374
  35.2 0.0 collective-permute-done.2.far_ref
  35.2 0.0 collective-permute-done.3.near_ref
  35.2 2.8 %shard_map.92 = (f32[20,32,128]{2,1,0:T(8,128)}, f32[512,128]{1,0:T(8,128)S(1)}) custom-call(f32[5,5]{1,0:T(8,128)S(1)} %copy-done.4, f32[20,32,128]{2,1,0:T(8,128)S(1)} %shard_map.90.main_ref, f32[48,128]{1,0:T(8,128)S(1)} %collective-permute-done.2.far_ref, f32[48,128]{1,0:T(8,128)S(1)} %collective-permute-done.3.near_ref, ...), custom_call_target="tpu_custom_call" | custom-call | flops 2000000 | bytes 1000000 | tf_op jit(solution)/shard_map/pallas_call | solution.py:403
  37.9 22.3 %all_to_all.5 = f32[32,16,128]{2,1,0:T(8,128)S(1)} all-to-all(f32[32,16,128]{2,1,0:T(8,128)S(1)} %bitcast.15), channel_id=1, replica_groups=mesh['grp'=4,'lat'=8,'lon'=32] {'lon'}, dimensions={0} | all-to-all | bytes 524288 | tf_op jit(solution)/shard_map/all_to_all | solution.py:413
  60.2 2.4 %shard_map.93 = (f32[5,128,128]{2,1,0:T(8,128)}, f32[12,128,128]{2,1,0:T(8,128)}) custom-call(f32[512,128]{1,0:T(8,128)S(1)} %bitcast.14, f32[5,128,128]{2,1,0:T(8,128)} %bitcast.18, f32[12,128,128]{2,1,0:T(8,128)S(1)} %bitcast.10, f32[12,128,128]{2,1,0:T(8,128)S(1)} %get-tuple-element.53.pre_ref), custom_call_target="tpu_custom_call", output_to_operand_aliasing={{0}: (1, {})} | custom-call | flops 10000000 | bytes 2500000 | tf_op jit(solution)/shard_map/pallas_call | solution.py:418
Async XLA Ops:
  0.6 1.0 %copy-start.2 = (f32[5,4,32,128]{3,2,1,0:T(8,128)S(1)}, f32[5,4,32,128]{3,2,1,0:T(8,128)}, u32[]{:S(2)}) copy-start(f32[5,4,32,128]{3,2,1,0:T(8,128)} %param.7) | copy-start | bytes 983044
  1.6 11.2 %copy-start.3 = (f32[5,4,32,128]{3,2,1,0:T(8,128)S(1)}, f32[5,4,32,128]{3,2,1,0:T(8,128)}, u32[]{:S(2)}) copy-start(f32[5,4,32,128]{3,2,1,0:T(8,128)} %param.7) | copy-start | bytes 983044
  1.8 9.1 %collective-permute-start = (f32[20,8,128]{2,1,0:T(8,128)S(1)}, f32[20,8,128]{2,1,0:T(8,128)S(1)}, u32[]{:S(2)}, u32[]{:S(2)}) collective-permute-start(f32[20,8,128]{2,1,0:T(8,128)S(1)} %get-tuple-element.29), channel_id=1, source_target_pairs={{0,32},{32,64},{64,96},{96,128},{128,160},{160,192},{192,224},{1,3... | collective-permute-start | bytes 245768 | tf_op jit(solution)/shard_map/ppermute | solution.py:355
  6.1 1.4 %copy-start.5 = (s32[24,3]{0,1:T(4,128)S(1)}, s32[24,3]{0,1:T(4,128)}, u32[]{:S(2)}) copy-start(s32[24,3]{0,1:T(4,128)} %param.11) | copy-start | bytes 868
  6.1 6.7 %collective-permute-start.1 = (f32[20,8,128]{2,1,0:T(8,128)S(1)}, f32[20,8,128]{2,1,0:T(8,128)S(1)}, u32[]{:S(2)}, u32[]{:S(2)}) collective-permute-start(f32[20,8,128]{2,1,0:T(8,128)S(1)} %get-tuple-element.30), channel_id=1, source_target_pairs={{32,0},{64,32},{96,64},{128,96},{160,128},{192,160},{224,192},{33,... | collective-permute-start | bytes 245768 | tf_op jit(solution)/shard_map/ppermute | solution.py:356
  7.4 0.7 %copy-start.6 = (f32[24]{0:T(128)S(1)}, f32[24]{0:T(128)}, u32[]{:S(2)}) copy-start(f32[24]{0:T(128)} %rates_ref.3) | copy-start | bytes 292
  7.4 0.7 %copy-start.7 = (s32[12]{0:T(128)S(1)}, s32[12]{0:T(128)}, u32[]{:S(2)}) copy-start(s32[12]{0:T(128)} %map_ref.3) | copy-start | bytes 148
  7.5 0.7 %copy-start.8 = (f32[4]{0:T(128)S(1)}, f32[4]{0:T(128)}, u32[]{:S(2)}) copy-start(f32[4]{0:T(128)} %coef_ref.3) | copy-start | bytes 52
  8.1 1.1 %copy-start = (f32[12,32,4,128]{3,2,1,0:T(4,128)S(1)}, f32[12,32,4,128]{3,2,1,0:T(4,128)}, u32[]{:S(2)}) copy-start(f32[12,32,4,128]{3,2,1,0:T(4,128)} %param.8) | copy-start | bytes 2359300
  9.3 3.6 %copy-start.4 = (f32[5,5]{1,0:T(8,128)S(1)}, f32[5,5]{1,0:T(8,128)}, u32[]{:S(2)}) copy-start(f32[5,5]{1,0:T(8,128)} %coupling_ref.5) | copy-start | bytes 304
  9.3 24.5 %copy-start.1 = (f32[12,32,4,128]{3,2,1,0:T(4,128)S(1)}, f32[12,32,4,128]{3,2,1,0:T(4,128)}, u32[]{:S(2)}) copy-start(f32[12,32,4,128]{3,2,1,0:T(4,128)} %param.8) | copy-start | bytes 2359300
  17.3 17.8 %collective-permute-start.2 = (f32[48,128]{1,0:T(8,128)S(1)}, f32[48,128]{1,0:T(8,128)S(1)}, u32[]{:S(2)}, u32[]{:S(2)}) collective-permute-start(f32[48,128]{1,0:T(8,128)S(1)} %get-tuple-element.46), channel_id=1, source_target_pairs={{0,768},{768,0},{256,512},{512,256},{1,769},{769,1},{257,513},{513... | collective-permute-start | bytes 73736 | tf_op jit(solution)/shard_map/ppermute | solution.py:398
  29.7 5.4 %collective-permute-start.3 = (f32[48,128]{1,0:T(8,128)S(1)}, f32[48,128]{1,0:T(8,128)S(1)}, u32[]{:S(2)}, u32[]{:S(2)}) collective-permute-start(f32[48,128]{1,0:T(8,128)S(1)} %get-tuple-element.47), channel_id=1, source_target_pairs={{0,256},{256,0},{512,768},{768,512},{1,257},{257,1},{513,769},{769... | collective-permute-start | bytes 73736 | tf_op jit(solution)/shard_map/ppermute | solution.py:399

commit v4 on v3

--- a/solution.py
+++ b/solution.py
@@ -37,9 +37,8 @@
     return jnp.where(odd, right, left), jnp.where(odd, left, right)
 
 
-def edge_kernel(state_ref, top_ref, bottom_ref, far_ref, near_ref):
-    top_ref[...] = state_ref[:, :BAND]
-    bottom_ref[...] = state_ref[:, ROWS - BAND :]
+def own_kernel(state_ref, *refs):
+    far_ref, near_ref = refs[-2:]
     far_ref[...], near_ref[...] = packed(state_ref)
 
 
@@ -52,16 +51,16 @@
 
 def regroup(chunks):
     lanes = lane_index(ROWS)
-    width = LANES // 4
-    out = []
-    for j in range(4):
-        total = None
+    chunks = list(chunks)
+    for bit in (2, 1):
+        width = bit * LANES // 4
+        lower = lax.rem(lanes // width, 2) == 0
         for i in range(4):
-            turn = (width * (i - j)) % LANES
-            moved = pltpu.roll(chunks[i], turn, 1) if turn else chunks[i]
-            total = moved if total is None else jnp.where(lanes >= width * i, moved, total)
-        out.append(total)
-    return out
+            if not i & bit:
+                a, b = chunks[i], chunks[i + bit]
+                chunks[i] = jnp.where(lower, a, pltpu.roll(b, width, 1))
+                chunks[i + bit] = jnp.where(lower, pltpu.roll(a, LANES - width, 1), b)
+    return chunks
 
 
 def runs_here(early):
@@ -69,19 +68,17 @@
     return first if early else jnp.logical_not(first)
 
 
-def chem_kernel(early, rates_ref, pairs_ref, map_ref, coef_ref, q_ref, *refs):
-    pre_ref, heat_ref, heat_sc, turn_sc = refs[-4:]
+def local_kernel(early, *refs):
+    inputs, outputs, scratch = refs[:9], refs[-13:-9], refs[-9:]
+    rates_ref, pairs_ref, map_ref, coef_ref, q_ref, coupling_ref, state_ref, low_ref, high_ref = inputs
+    pre_ref, heat_ref, main_ref, send_ref = outputs
 
     @pl.when(runs_here(early))
     def _():
-        chemistry(rates_ref, pairs_ref, map_ref, coef_ref, q_ref, pre_ref, heat_ref, heat_sc, turn_sc)
-
-    if not early:
-
-        @pl.when(runs_here(True))
-        def _():
-            pre_ref[...] = refs[0][...]
-            heat_ref[...] = refs[1][...]
+        whole_step(coupling_ref, state_ref, low_ref, high_ref, main_ref, send_ref, *scratch[:6], scratch[8])
+        chemistry(rates_ref, pairs_ref, map_ref, coef_ref, q_ref, pre_ref, heat_ref, *scratch[6:8])
+        for y in range(4):
+            send_ref[pl.ds(12 + y, PEERS, stride=SLOTS), :] = heat_ref[y]
 
 
 def chemistry(rates_ref, pairs_ref, map_ref, coef_ref, q_ref, pre_ref, heat_ref, heat_sc, turn_sc):
@@ -113,21 +110,7 @@
     return lat > 0, lat < lax.axis_size("lat") - 1
 
 
-def rk_kernel(early, coupling_ref, state_ref, low_ref, high_ref, *refs):
-    out_ref = refs[-7]
-
-    @pl.when(runs_here(early))
-    def _():
-        whole_step(coupling_ref, state_ref, low_ref, high_ref, *refs[-7:])
-
-    if not early:
-
-        @pl.when(runs_here(True))
-        def _():
-            out_ref[...] = refs[0][...]
-
-
-def whole_step(coupling_ref, state_ref, low_ref, high_ref, out_ref, sa, sb, ta, tb, ua, ub):
+def whole_step(coupling_ref, state_ref, low_ref, high_ref, out_ref, send_ref, sa, sb, ta, tb, ua, ub, turn_sc):
     has_low, has_high = lat_ends()
     base = 16
 
@@ -207,9 +190,16 @@
     lax.fori_loop(0, LEVELS, stage_two, 0)
     lax.fori_loop(0, LEVELS, stage_three, 0)
 
+    for f in range(3):
+        plane = jnp.concatenate([out_ref[f * LEVELS + z] for z in range(LEVELS)], 0)
+        turn_sc[f] = jnp.transpose(plane)
+        chunks = [turn_sc[f, pl.ds(y, PEERS, stride=4), :] for y in range(4)]
+        for level, block in enumerate(regroup(chunks)):
+            send_ref[pl.ds(4 * f + level, PEERS, stride=SLOTS), :] = block
+
 
 def edge_step_kernel(
-    coupling_ref, main_ref, far_ref, near_ref, heat_ref, out_ref, send_ref, sa, sb, ta, tb, ua, ub, turn_sc
+    once_ref, twice_ref, main_ref, sent_ref, far_ref, near_ref, out_ref, send_ref, sa, sb, ta, tb, ua, ub, turn_sc
 ):
     odd = lax.rem(lax.axis_index("grp"), 2) == 1
     has_low, has_high = lat_ends()
@@ -223,34 +213,47 @@
     lanes = lane_index(8)
     column = lax.rem(lanes, HALO)
     field = lanes // (HALO * LEVELS)
-    mixes = {}
-    for d in range(1 - FIELDS, FIELDS):
-        total = jnp.zeros((8, LANES), jnp.float32)
-        for f in range(max(d, 0), min(FIELDS, FIELDS + d)):
-            total = jnp.where(field == f, coupling_ref[f, f - d] + (0.6 if d == 0 else 0.0), total)
-        mixes[d] = total
+
+    def mix_of(ref):
+        mixes = {}
+        for d in range(1 - FIELDS, FIELDS):
+            total = jnp.zeros((8, LANES), jnp.float32)
+            for f in range(max(d, 0), min(FIELDS, FIELDS + d)):
+                total = jnp.where(field == f, ref[f, f - d], total)
+            mixes[d] = total
+        return mixes
+
+    once, twice = mix_of(once_ref), mix_of(twice_ref)
 
     def turn(value, by):
         return pltpu.roll(value, by % LANES, 1) if by % LANES else value
 
-    def apply(a_ref, b_ref, row):
+    def apply(a_ref, b_ref, row, parts="ab"):
         a, b = a_ref[row : row + 8, :], b_ref[row : row + 8, :]
-        ya, yb = {}, {}
-        for j in (1, 2):
-            inside, behind = column < HALO - j, column >= j
-            ya[j] = jnp.where(inside, turn(a, -j), turn(b, HALO - j))
-            yb[j] = jnp.where(inside, turn(b, -j), 0.0)
-            ya[-j] = jnp.where(behind, turn(a, j), 0.0)
-            yb[-j] = jnp.where(behind, turn(b, j), turn(a, j - HALO))
         out = []
-        for value, ref, y in ((a, a_ref, ya), (b, b_ref, yb)):
+        for part in parts:
+            y = {}
+            for j in (1, 2):
+                inside, behind = column < HALO - j, column >= j
+                if part == "a":
+                    y[j] = jnp.where(inside, turn(a, -j), turn(b, HALO - j))
+                    y[-j] = jnp.where(behind, turn(a, j), 0.0)
+                else:
+                    y[j] = jnp.where(inside, turn(b, -j), 0.0)
+                    y[-j] = jnp.where(behind, turn(b, j), turn(a, j - HALO))
+            ref = a_ref if part == "a" else b_ref
             x = {j: ref[row + j : row + j + 8, :] for j in (1, 2, -1, -2)}
             total = -0.1 * (x[1] + y[1]) + 0.3 * (x[-1] + y[-1])
             total = total + 0.025 * ((x[2] - x[-2]) + (y[2] - y[-2]))
-            for d, mix in mixes.items():
-                total = total + mix * turn(value, HALO * LEVELS * d)
-            out.append(total)
+            out.append(total - 0.4 * (a if part == "a" else b))
         return out
+
+    def mixed(mixes, value):
+        total = None
+        for d, mix in mixes.items():
+            term = mix * turn(value, HALO * LEVELS * d)
+            total = term if total is None else total + term
+        return total
 
     def masked(value, row):
         place = (row - pad) % SPAN
@@ -267,32 +270,50 @@
         tb[row : row + 8, :] = masked(b, row)
     for row in every:
         a, b = apply(ta, tb, row)
-        ua[row : row + 8, :] = masked(0.75 * sa[row : row + 8, :] + 0.25 * a, row)
-        ub[row : row + 8, :] = masked(0.75 * sb[row : row + 8, :] + 0.25 * b, row)
+        ua[row : row + 8, :] = masked(a, row)
+        ub[row : row + 8, :] = masked(b, row)
+    firsts, finals = [], []
     for row in range(pad + BAND, pad + BAND + ROWS, 8):
-        _, b = apply(ua, ub, row)
-        a, _ = apply(ua, ub, row + SPAN)
-        first, final = (2.0 / 3.0) * b, (2.0 / 3.0) * a
+        (b,) = apply(ua, ub, row, "b")
+        (a,) = apply(ua, ub, row + SPAN, "a")
+        first = mixed(twice, tb[row : row + 8, :]) + mixed(once, 0.5 * ub[row : row + 8, :]) + b * (1.0 / 6.0)
+        other = row + SPAN
+        final = mixed(twice, ta[other : other + 8, :]) + mixed(once, 0.5 * ua[other : other + 8, :]) + a * (1.0 / 6.0)
+        firsts.append(first)
+        finals.append(final)
         place = row - pad - BAND
         for plane in range(PLANES):
             gain = jnp.where(lanes < HALO, turn(first, -HALO * plane), 0.0)
             gain = jnp.where(lanes >= LANES - HALO, turn(final, LANES - HALO - HALO * plane), gain)
             out_ref[plane, place : place + 8, :] = main_ref[plane, place : place + 8, :] + gain
 
-    for f in range(3):
-        plane = jnp.concatenate([out_ref[f * LEVELS + z] for z in range(LEVELS)], 0)
-        turn_sc[f] = jnp.transpose(plane)
-        chunks = [turn_sc[f, pl.ds(y, PEERS, stride=4), :] for y in range(4)]
-        for level, block in enumerate(regroup(chunks)):
-            send_ref[pl.ds(4 * f + level, PEERS, stride=SLOTS), :] = block
-    for y in range(4):
-        send_ref[pl.ds(12 + y, PEERS, stride=SLOTS), :] = heat_ref[y]
-
-
-def final_kernel(recv_ref, temp_ref, q_ref, pre_ref, temp_out_ref, q_out_ref, turn_sc, wind_sc):
-    for y in range(4):
-        turn_sc[pl.ds(y, PEERS, stride=4), :] = recv_ref[pl.ds(12 + y, PEERS, stride=SLOTS), :]
-    temp_out_ref[0] = temp_ref[0] + 0.5 * jnp.transpose(turn_sc[...])
+    send_ref[...] = sent_ref[...]
+    winds = 3 * LEVELS
+    lanes12 = lane_index(winds)
+    zeros = jnp.zeros((LANES - ROWS, LANES), jnp.float32)
+    for side, values in ((0, firsts), (1, finals)):
+        turn_sc[side] = jnp.transpose(jnp.concatenate(values + [zeros], 0))
+        for peer in (0, 1) if side == 0 else (PEERS - 2, PEERS - 1):
+            gain = jnp.zeros((winds, LANES), jnp.float32)
+            for y in range(4):
+                c = 4 * peer + y - (LANES - HALO if side else 0)
+                if 0 <= c < HALO:
+                    part = turn_sc[side, pl.ds(c, winds, stride=HALO), :]
+                    here = jnp.logical_and(lanes12 >= ROWS * y, lanes12 < ROWS * y + ROWS)
+                    gain = jnp.where(here, turn(part, ROWS * y), gain)
+            send_ref[peer * SLOTS : peer * SLOTS + winds, :] += gain
+
+
+def final_kernel(recv_ref, stepped_ref, q_ref, pre_ref, state_out_ref, q_out_ref, turn_sc, wind_sc, temp_sc, q_sc, sems):
+    copies = []
+
+    def send_out(source, target):
+        copy = pltpu.make_async_copy(source, target, sems.at[len(copies)])
+        copy.start()
+        copies.append(copy)
+
+    send_out(stepped_ref.at[0:3], state_out_ref.at[0:3])
+    send_out(stepped_ref.at[4:5], state_out_ref.at[4:5])
     for f in range(3):
         for level in range(4):
             turn_sc[pl.ds(level, PEERS, stride=4), :] = recv_ref[pl.ds(4 * f + level, PEERS, stride=SLOTS), :]
@@ -323,7 +344,15 @@
         for s in range(SPECIES):
             value = q_ref[s, rows, :]
             higher, lower = clamped(value)
-            q_out_ref[s, rows, :] = pre_ref[s, rows, :] + (up * (higher - value) - down * (value - lower))
+            q_sc[s, rows, :] = pre_ref[s, rows, :] + (up * (higher - value) - down * (value - lower))
+        send_out(q_sc.at[:, rows, :], q_out_ref.at[:, rows, :])
+        if start == 0:
+            for y in range(4):
+                turn_sc[pl.ds(y, PEERS, stride=4), :] = recv_ref[pl.ds(12 + y, PEERS, stride=SLOTS), :]
+            temp_sc[0] = stepped_ref[3] + 0.5 * jnp.transpose(turn_sc[...])
+            send_out(temp_sc, state_out_ref.at[3:4])
+    for copy in copies:
+        copy.wait()
 
 
 VMEM = pl.BlockSpec(memory_space=pltpu.VMEM)
@@ -343,49 +372,44 @@
     planes = state.reshape(PLANES, ROWS, LANES)
     q = tracers.reshape(SPECIES, 128, 128)
 
-    top, bottom, own_far, own_near = pl.pallas_call(
-        edge_kernel,
-        out_shape=(shape(PLANES, BAND, LANES),) * 2 + (shape(ROWS, LANES),) * 2,
-        in_specs=[VMEM],
-        out_specs=(VMEM,) * 4,
-        cost_estimate=cost(1000000, 500000),
+    count = lax.axis_size("lat")
+    low = lax.ppermute(planes[:, ROWS - BAND :], "lat", [(i, i + 1) for i in range(count - 1)])
+    high = lax.ppermute(planes[:, :BAND], "lat", [(i + 1, i) for i in range(count - 1)])
+    once = jnp.eye(FIELDS, dtype=jnp.float32) + coupling
+    squared = jnp.sum(coupling[:, :, None] * coupling[None, :, :], 1)
+    twice = once + 0.5 * squared
+    reactants = (rates, pairs.T, heat_map, heat_coef, q)
+
+    own_far, own_near = pl.pallas_call(
+        own_kernel,
+        out_shape=(shape(ROWS, LANES),) * 2,
+        in_specs=[VMEM] + [SMEM] * 4 + [VMEM, SMEM],
+        out_specs=(VMEM,) * 2,
+        cost_estimate=cost(1000000, 400000),
         compiler_params=PARAMS,
-    )(planes)
-    count = lax.axis_size("lat")
-    low = lax.ppermute(bottom, "lat", [(i, i + 1) for i in range(count - 1)])
-    high = lax.ppermute(top, "lat", [(i + 1, i) for i in range(count - 1)])
-    reactants = (rates, pairs.T, heat_map, heat_coef, q)
-
-    def chem(early, *before):
+    )(planes, *reactants, coupling)
+    extended = pltpu.VMEM((PLANES, 64, LANES), jnp.float32)
+    square = pltpu.VMEM((128, 128), jnp.float32)
+
+    def local(early, *before):
         return pl.pallas_call(
-            functools.partial(chem_kernel, early),
-            out_shape=(shape(SPECIES, 128, 128), shape(4, PEERS, LANES)),
-            in_specs=[SMEM, SMEM, SMEM, SMEM, VMEM] + [VMEM] * len(before),
-            out_specs=(VMEM, VMEM),
-            scratch_shapes=[pltpu.VMEM((128, 128), jnp.float32), pltpu.VMEM((128, 128), jnp.float32)],
-            input_output_aliases={5 + i: i for i in range(len(before))},
-            cost_estimate=cost(10000000, 2000000),
+            functools.partial(local_kernel, early),
+            out_shape=(
+                shape(SPECIES, 128, 128),
+                shape(4, PEERS, LANES),
+                shape(PLANES, ROWS, LANES),
+                shape(PEERS * SLOTS, LANES),
+            ),
+            in_specs=[SMEM] * 4 + [VMEM, SMEM] + [VMEM] * (3 + len(before)),
+            out_specs=(VMEM,) * 4,
+            scratch_shapes=[extended] * 6 + [square] * 2 + [pltpu.VMEM((3, 128, 128), jnp.float32)],
+            input_output_aliases={9 + i: i for i in range(len(before))},
+            cost_estimate=cost(30000000, 3000000),
             compiler_params=PARAMS,
-        )(*reactants, *before)
-
-    extended = pltpu.VMEM((PLANES, 64, LANES), jnp.float32)
-
-    def rk(early, *before):
-        return pl.pallas_call(
-            functools.partial(rk_kernel, early),
-            out_shape=shape(PLANES, ROWS, LANES),
-            in_specs=[SMEM] + [VMEM] * (3 + len(before)),
-            out_specs=VMEM,
-            scratch_shapes=[extended] * 6,
-            input_output_aliases={4 + i: i for i in range(len(before))},
-            cost_estimate=cost(20000000, 1500000),
-            compiler_params=PARAMS,
-        )(coupling, planes, low, high, *before)
-
-    pre, heat = chem(True)
-    low, high, heat = lax.optimization_barrier((low, high, heat))
-    main = rk(True)
-    low, high, main = lax.optimization_barrier((low, high, main))
+        )(*reactants, coupling, planes, low, high, *before)
+
+    done = local(True)
+    low, high, once, twice, *done = lax.optimization_barrier((low, high, once, twice, *done))
     far, near = pl.pallas_call(
         pack_kernel,
         out_shape=(shape(SPAN, LANES), shape(SPAN, LANES)),
@@ -394,35 +418,38 @@
         cost_estimate=cost(1000000, 400000),
         compiler_params=PARAMS,
     )(low, high, own_far, own_near)
-    far, near, low, high, main, pre, heat = lax.optimization_barrier((far, near, low, high, main, pre, heat))
+    far, near, low, high, *done = lax.optimization_barrier((far, near, low, high, *done))
     far_in = lax.ppermute(far, "grp", [(0, 3), (3, 0), (1, 2), (2, 1)])
     near_in = lax.ppermute(near, "grp", [(0, 1), (1, 0), (2, 3), (3, 2)])
-    pre, heat = chem(False, pre, heat)
-    main = rk(False, main)
+    pre, _, main, sent = local(False, *done)
     window = pltpu.VMEM((2 * SPAN + 16, LANES), jnp.float32)
     stepped, send = pl.pallas_call(
         edge_step_kernel,
         out_shape=(shape(PLANES, ROWS, LANES), shape(PEERS * SLOTS, LANES)),
-        in_specs=[SMEM] + [VMEM] * 4,
+        in_specs=[SMEM] * 2 + [VMEM] * 4,
         out_specs=(VMEM, VMEM),
-        scratch_shapes=[window] * 6 + [pltpu.VMEM((3, 128, 128), jnp.float32)],
+        scratch_shapes=[window] * 6 + [pltpu.VMEM((2, 128, 128), jnp.float32)],
+        input_output_aliases={3: 1},
         cost_estimate=cost(2000000, 1000000),
         compiler_params=PARAMS,
-    )(coupling, main, far_in, near_in, heat)
+    )(once, twice, main, sent, far_in, near_in)
 
     received = lax.all_to_all(
         send.reshape(PEERS, SLOTS, LANES), "lon", split_axis=0, concat_axis=0, tiled=True
     )
-    temperature = pl.BlockSpec((1, 128, 128), lambda i: (3, 0, 0))
-    whole = pl.BlockSpec((SPECIES, 128, 128), lambda i: (0, 0, 0))
+    outside = pl.BlockSpec(memory_space=pltpu.HBM)
     state_out, q_out = pl.pallas_call(
         final_kernel,
-        grid=(1,),
         out_shape=(shape(FIELDS, 128, 128), shape(SPECIES, 128, 128)),
-        in_specs=[pl.BlockSpec((PEERS * SLOTS, LANES), lambda i: (0, 0)), temperature, whole, whole],
-        out_specs=(temperature, whole),
-        scratch_shapes=[pltpu.VMEM((128, 128), jnp.float32), pltpu.VMEM((3, 128, 128), jnp.float32)],
-        input_output_aliases={1: 0},
+        in_specs=[VMEM] * 4,
+        out_specs=(outside,) * 2,
+        scratch_shapes=[
+            square,
+            pltpu.VMEM((3, 128, 128), jnp.float32),
+            pltpu.VMEM((1, 128, 128), jnp.float32),
+            pltpu.VMEM((SPECIES, 128, 128), jnp.float32),
+            pltpu.SemaphoreType.DMA((7,)),
+        ],
         cost_estimate=cost(10000000, 2500000),
         compiler_params=PARAMS,
     )(received.reshape(PEERS * SLOTS, LANES), stepped.reshape(FIELDS, 128, 128), q, pre)

time: 63.1 us -> 60.4 us (0.957)
  Pallas kernels: 13 us -> 10.7 us
  waiting for transfers between devices: 1.87 us -> 0.13 us
  blocking collectives: 22.3 us -> 23.4 us
    ppermute x2, waiting for transfers between devices: 1.87 us -> 0.01 us  [the longest x1 0.01 us: on_device(): lax.ppermute(planes[:, :BAND], 'lat', [(i + 1, i) for i in range(count -...]
    pallas_call x6 -> x4, Pallas kernels: 10 us -> 8.87 us  [the longest x2 6.54 us: local(): pl.pallas_call(functools.partial(local_kernel, early), out_shape=(shape(S...]
    all_to_all x1, blocking collectives: 22.3 us -> 23.4 us  [on_device(): lax.all_to_all(send.reshape(PEERS, SLOTS, LANES), 'lon', split_axis=0, co...]
    pallas_call x1, Pallas kernels: 2.77 us -> 1.73 us  [on_device(): pl.pallas_call(edge_step_kernel, out_shape=(shape(PLANES, ROWS, LANES), s...]
    slice x0 -> x1, local copies, waits for them, and re-layouts: none -> 0.99 us  [on_device(): planes[:, :BAND]]
    unnamed x18 -> x16, local copies, waits for them, and re-layouts: 2.77 us -> 1.81 us
    ppermute x1, starting transfers between devices: 4.01 us -> 3.14 us  [on_device(): near_in = lax.ppermute(near, 'grp', [(0, 1), (1, 0), (2, 3), (3, 2)])]
  transfers between devices with their start and end apart: 4 -> 4, of which waited for: 1 -> 1; matrix products, arithmetic and copies ran while one was open for 0% -> 0% of each run, Pallas kernels for 5% -> 3%
where the time goes in v4:
time: 60.4 us; the launch traced here: 60.1 us
  blocking collectives  23.4 us (39%)
  starting transfers between devices  22 us (36%)
  Pallas kernels  10.7 us (18%)
  local copies, waits for them, and re-layouts  2.8 us (5%)
  between operations  0.81 us (1%)
    all_to_all x1, blocking collectives, on_device(): lax.all_to_all(send.reshape(PEERS, SLOTS, LANES), 'lon', split_axis=0, co...  23.4 us
    ppermute x1, starting transfers between devices, on_device(): far_in = lax.ppermute(far, 'grp', [(0, 3), (3, 0), (1, 2), (2, 1)])  12.7 us
    pallas_call x2, Pallas kernels, local(): pl.pallas_call(functools.partial(local_kernel, early), out_shape=(shape(S...  6.54 us
    ppermute x1, starting transfers between devices, on_device(): lax.ppermute(planes[:, ROWS - BAND:], 'lat', [(i, i + 1) for i in range(c...  4.91 us
    ppermute x1, starting transfers between devices, on_device(): near_in = lax.ppermute(near, 'grp', [(0, 1), (1, 0), (2, 3), (3, 2)])  3.14 us
    unnamed x16, local copies, waits for them, and re-layouts  1.81 us
    pallas_call x1, Pallas kernels, on_device(): pl.pallas_call(edge_step_kernel, out_shape=(shape(PLANES, ROWS, LANES), s...  1.73 us
    pallas_call x1, Pallas kernels, on_device(): pl.pallas_call(final_kernel, out_shape=(shape(FIELDS, 128, 128), shape(SP...  1.45 us
  transfers between devices with their start and end apart: 4, of which 1 were waited for; matrix products, arithmetic and copies ran while one was open for 0% of the time, Pallas kernels for 3%

profile of v4, /device:TPU:8, one launch (start us, length us, event | category | flops | bytes accessed | tf_op | source)
XLA Modules:
  0.0 60.1 jit_solution(16344033742425543752)
XLA Ops:
  0.6 0.0 copy-start.2
  0.6 0.0 copy-start.3
  0.6 1.0 %fusion = (f32[20,8,128]{2,1,0:T(8,128)S(1)}, f32[20,8,128]{2,1,0:T(8,128)S(1)}) fusion(f32[20,32,128]{2,1,0:T(8,128)} %bitcast.12), kind=kLoop, calls=%fused_computation.4 | loop fusion | bytes 327680 | tf_op jit(solution)/shard_map/slice | solution.py:377
  1.6 1.3 %collective-permute-start.1 = (f32[20,8,128]{2,1,0:T(8,128)S(1)}, f32[20,8,128]{2,1,0:T(8,128)S(1)}, u32[]{:S(2)}, u32[]{:S(2)}) collective-permute-start(f32[20,8,128]{2,1,0:T(8,128)S(1)} %get-tuple-element.64), channel_id=1, source_target_pairs={{32,0},{64,32},{96,64},{128,96},{160,128},{192,160},{224,192},{33,... | collective-permute-start | bytes 245768 | tf_op jit(solution)/shard_map/ppermute | solution.py:377
  2.9 4.9 %collective-permute-start = (f32[20,8,128]{2,1,0:T(8,128)S(1)}, f32[20,8,128]{2,1,0:T(8,128)S(1)}, u32[]{:S(2)}, u32[]{:S(2)}) collective-permute-start(f32[20,8,128]{2,1,0:T(8,128)S(1)} %get-tuple-element.65), channel_id=1, source_target_pairs={{0,32},{32,64},{64,96},{96,128},{128,160},{160,192},{192,224},{1,3... | collective-permute-start | bytes 245768 | tf_op jit(solution)/shard_map/ppermute | solution.py:376
  7.9 0.0 copy-done.3
  7.9 0.1 multiply_reduce_fusion
  8.0 0.0 copy-start.4
  8.0 0.0 copy-start.5
  8.0 0.0 copy-start.6
  8.0 0.0 copy-start.7
  8.0 0.0 copy-done.2
  8.0 0.6 %copy-done.4 = s32[24,3]{0,1:T(4,128)S(1)} copy-done((s32[24,3]{0,1:T(4,128)S(1)}, s32[24,3]{0,1:T(4,128)}, u32[]{:S(2)}) %copy-start.4) | copy-done | bytes 312
  8.7 0.0 copy-done.5
  8.7 0.0 copy-done.6
  8.7 0.0 copy-done.7
  8.7 0.0 copy-start
  8.7 1.1 %copy-done = f32[12,32,4,128]{3,2,1,0:T(4,128)S(1)} copy-done((f32[12,32,4,128]{3,2,1,0:T(4,128)S(1)}, f32[12,32,4,128]{3,2,1,0:T(4,128)}, u32[]{:S(2)}) %copy-start) | copy-done | bytes 786456
  9.8 0.9 %shard_map.87 = (f32[32,128]{1,0:T(8,128)S(1)}, f32[32,128]{1,0:T(8,128)S(1)}) custom-call(f32[20,32,128]{2,1,0:T(8,128)S(1)} %bitcast.13, f32[24]{0:T(128)S(1)} %copy-done.5, s32[3,24]{1,0:T(4,128)S(1)} %bitcast.19, s32[12]{0:T(128)S(1)} %copy-done.6, f32[4]{0:T(128)S(1)} %copy-done.7, f32[12,128,128]{2,1,0:T(8,128)S(1)} %bitcast.8, f32[5,5]{1,0:T(8,128)S(1)} %copy-done.3), custom_call_target="tpu_custom_call" | custom-call | flops 1000000 | bytes 400000 | tf_op jit(solution)/shard_map/pallas_call | solution.py:383
  10.7 0.0 copy-start.1
  10.7 0.0 collective-permute-done.1.refs_8_.high_ref
  10.7 0.0 collective-permute-done.refs_7_.low_ref
  10.7 5.9 %shard_map.86 = (f32[12,128,128]{2,1,0:T(8,128)S(1)}, f32[4,32,128]{2,1,0:T(8,128)S(1)}, f32[20,32,128]{2,1,0:T(8,128)S(1)}, f32[512,128]{1,0:T(8,128)S(1)}) custom-call(f32[24]{0:T(128)S(1)} %copy-done.5, s32[3,24]{1,0:T(4,128)S(1)} %bitcast.20, s32[12]{0:T(128)S(1)} %copy-done.6, f32[4]{0:T(128)S(1)} %copy-done.7, f32[12,128,128]{2,1,0:T(8,128)S(1)} %bitcast.9, ...), custom_call_target="tpu_custom_call" | custom-call | flops 30000000 | bytes 3000000 | tf_op jit(solution)/shard_map/pallas_call | solution.py:395
  16.6 0.1 shard_map.88
  16.8 12.7 %collective-permute-start.2 = (f32[48,128]{1,0:T(8,128)S(1)}, f32[48,128]{1,0:T(8,128)S(1)}, u32[]{:S(2)}, u32[]{:S(2)}) collective-permute-start(f32[48,128]{1,0:T(8,128)S(1)} %get-tuple-element.57), channel_id=1, source_target_pairs={{0,768},{768,0},{256,512},{512,256},{1,769},{769,1},{257,513},{513... | collective-permute-start | bytes 73736 | tf_op jit(solution)/shard_map/ppermute | solution.py:422
  29.5 3.1 %collective-permute-start.3 = (f32[48,128]{1,0:T(8,128)S(1)}, f32[48,128]{1,0:T(8,128)S(1)}, u32[]{:S(2)}, u32[]{:S(2)}) collective-permute-start(f32[48,128]{1,0:T(8,128)S(1)} %get-tuple-element.58), channel_id=1, source_target_pairs={{0,256},{256,0},{512,768},{768,512},{1,257},{257,1},{513,769},{769... | collective-permute-start | bytes 73736 | tf_op jit(solution)/shard_map/ppermute | solution.py:423
  32.6 0.0 copy-done.1
  32.6 0.7 %shard_map.89 = (f32[12,128,128]{2,1,0:T(8,128)S(1)}, f32[4,32,128]{2,1,0:T(8,128)S(1)}, f32[20,32,128]{2,1,0:T(8,128)S(1)}, f32[512,128]{1,0:T(8,128)S(1)}) custom-call(f32[24]{0:T(128)S(1)} %copy-done.5, s32[3,24]{1,0:T(4,128)S(1)} %bitcast.21, s32[12]{0:T(128)S(1)} %copy-done.6, ...), custom_call_target="tpu_custom_call", output_to_operand_aliasing={{0}: (9, {}), {1}: (10, {}), {2}: (11, {}), {3}: (12, {})} | custom-call | flops 30000000 | bytes 3000000 | tf_op jit(solution)/shard_map/pallas_call | solution.py:395
  33.3 0.0 collective-permute-done.2.far_ref
  33.3 0.1 collective-permute-done.3.near_ref
  33.4 1.7 %shard_map.90 = (f32[20,32,128]{2,1,0:T(8,128)S(1)}, f32[512,128]{1,0:T(8,128)S(1)}) custom-call(f32[5,5]{1,0:T(8,128)S(1)} %get-tuple-element.37.once_ref, f32[5,5]{1,0:T(8,128)S(1)} %get-tuple-element.38.twice_ref, f32[20,32,128]{2,1,0:T(8,128)S(1)} %get-tuple-element.55.main_ref, ...), custom_call_target="tpu_custom_call", output_to_operand_aliasing={{1}: (3, {})} | custom-call | flops 2000000 | bytes 1000000 | tf_op jit(solution)/shard_map/pallas_call | solution.py:426
  35.2 23.4 %all_to_all.5 = f32[32,16,128]{2,1,0:T(8,128)S(1)} all-to-all(f32[32,16,128]{2,1,0:T(8,128)S(1)} %bitcast.16), channel_id=1, replica_groups=mesh['grp'=4,'lat'=8,'lon'=32] {'lon'}, dimensions={0} | all-to-all | bytes 524288 | tf_op jit(solution)/shard_map/all_to_all | solution.py:437
  58.6 1.4 %shard_map.91 = (f32[5,128,128]{2,1,0:T(8,128)}, f32[12,128,128]{2,1,0:T(8,128)}) custom-call(f32[512,128]{1,0:T(8,128)S(1)} %bitcast.17, f32[5,128,128]{2,1,0:T(8,128)S(1)} %bitcast.18, f32[12,128,128]{2,1,0:T(8,128)S(1)} %bitcast.11, f32[12,128,128]{2,1,0:T(8,128)S(1)} %get-tuple-element.61.pre_ref), custom_call_target="tpu_custom_call" | custom-call | flops 10000000 | bytes 2500000 | tf_op jit(solution)/shard_map/pallas_call | solution.py:441
  (1 shorter events, 0.0 us)
Async XLA Ops:
  0.6 7.4 %copy-start.2 = (f32[5,4,32,128]{3,2,1,0:T(8,128)S(1)}, f32[5,4,32,128]{3,2,1,0:T(8,128)}, u32[]{:S(2)}) copy-start(f32[5,4,32,128]{3,2,1,0:T(8,128)} %param.7) | copy-start | bytes 983044
  0.6 7.2 %copy-start.3 = (f32[5,5]{1,0:T(8,128)S(1)}, f32[5,5]{1,0:T(8,128)}, u32[]{:S(2)}) copy-start(f32[5,5]{1,0:T(8,128)} %refs_5_.5) | copy-start | bytes 304
  1.6 9.1 %collective-permute-start.1 = (f32[20,8,128]{2,1,0:T(8,128)S(1)}, f32[20,8,128]{2,1,0:T(8,128)S(1)}, u32[]{:S(2)}, u32[]{:S(2)}) collective-permute-start(f32[20,8,128]{2,1,0:T(8,128)S(1)} %get-tuple-element.64), channel_id=1, source_target_pairs={{32,0},{64,32},{96,64},{128,96},{160,128},{192,160},{224,192},{33,... | collective-permute-start | bytes 245768 | tf_op jit(solution)/shard_map/ppermute | solution.py:377
  2.9 7.8 %collective-permute-start = (f32[20,8,128]{2,1,0:T(8,128)S(1)}, f32[20,8,128]{2,1,0:T(8,128)S(1)}, u32[]{:S(2)}, u32[]{:S(2)}) collective-permute-start(f32[20,8,128]{2,1,0:T(8,128)S(1)} %get-tuple-element.65), channel_id=1, source_target_pairs={{0,32},{32,64},{64,96},{96,128},{128,160},{160,192},{192,224},{1,3... | collective-permute-start | bytes 245768 | tf_op jit(solution)/shard_map/ppermute | solution.py:376
  8.0 0.7 %copy-start.4 = (s32[24,3]{0,1:T(4,128)S(1)}, s32[24,3]{0,1:T(4,128)}, u32[]{:S(2)}) copy-start(s32[24,3]{0,1:T(4,128)} %param.11) | copy-start | bytes 868
  8.0 0.7 %copy-start.5 = (f32[24]{0:T(128)S(1)}, f32[24]{0:T(128)}, u32[]{:S(2)}) copy-start(f32[24]{0:T(128)} %refs_0_.5) | copy-start | bytes 292
  8.0 0.7 %copy-start.6 = (s32[12]{0:T(128)S(1)}, s32[12]{0:T(128)}, u32[]{:S(2)}) copy-start(s32[12]{0:T(128)} %refs_2_.5) | copy-start | bytes 148
  8.0 0.7 %copy-start.7 = (f32[4]{0:T(128)S(1)}, f32[4]{0:T(128)}, u32[]{:S(2)}) copy-start(f32[4]{0:T(128)} %refs_3_.5) | copy-start | bytes 52
  8.7 1.1 %copy-start = (f32[12,32,4,128]{3,2,1,0:T(4,128)S(1)}, f32[12,32,4,128]{3,2,1,0:T(4,128)}, u32[]{:S(2)}) copy-start(f32[12,32,4,128]{3,2,1,0:T(4,128)} %param.8) | copy-start | bytes 2359300
  10.7 21.9 %copy-start.1 = (f32[12,32,4,128]{3,2,1,0:T(4,128)S(1)}, f32[12,32,4,128]{3,2,1,0:T(4,128)}, u32[]{:S(2)}) copy-start(f32[12,32,4,128]{3,2,1,0:T(4,128)} %param.8) | copy-start | bytes 2359300
  16.8 16.5 %collective-permute-start.2 = (f32[48,128]{1,0:T(8,128)S(1)}, f32[48,128]{1,0:T(8,128)S(1)}, u32[]{:S(2)}, u32[]{:S(2)}) collective-permute-start(f32[48,128]{1,0:T(8,128)S(1)} %get-tuple-element.57), channel_id=1, source_target_pairs={{0,768},{768,0},{256,512},{512,256},{1,769},{769,1},{257,513},{513... | collective-permute-start | bytes 73736 | tf_op jit(solution)/shard_map/ppermute | solution.py:422
  29.5 4.0 %collective-permute-start.3 = (f32[48,128]{1,0:T(8,128)S(1)}, f32[48,128]{1,0:T(8,128)S(1)}, u32[]{:S(2)}, u32[]{:S(2)}) collective-permute-start(f32[48,128]{1,0:T(8,128)S(1)} %get-tuple-element.58), channel_id=1, source_target_pairs={{0,256},{256,0},{512,768},{768,512},{1,257},{257,1},{513,769},{769... | collective-permute-start | bytes 73736 | tf_op jit(solution)/shard_map/ppermute | solution.py:423

commit v5 on v4

--- a/solution.py
+++ b/solution.py
@@ -37,8 +37,7 @@
     return jnp.where(odd, right, left), jnp.where(odd, left, right)
 
 
-def own_kernel(state_ref, *refs):
-    far_ref, near_ref = refs[-2:]
+def own_kernel(state_ref, far_ref, near_ref):
     far_ref[...], near_ref[...] = packed(state_ref)
 
 
@@ -64,19 +63,27 @@
 
 
 def runs_here(early):
-    first = lax.axis_index("grp") < lax.axis_size("grp") // 2
+    grp, lat, lon = (lax.axis_index(axis) for axis in ("grp", "lat", "lon"))
+    held = jnp.logical_and(grp + lon == 0, lat < 3)
+    first = jnp.logical_and(grp < lax.axis_size("grp") // 2, jnp.logical_not(held))
     return first if early else jnp.logical_not(first)
 
 
 def local_kernel(early, *refs):
-    inputs, outputs, scratch = refs[:9], refs[-13:-9], refs[-9:]
-    rates_ref, pairs_ref, map_ref, coef_ref, q_ref, coupling_ref, state_ref, low_ref, high_ref = inputs
+    inputs, outputs, scratch, sems = refs[:9], refs[-20:-16], refs[-16:-1], refs[-1]
+    state_ref, low_ref, high_ref = inputs[6:]
     pre_ref, heat_ref, main_ref, send_ref = outputs
 
     @pl.when(runs_here(early))
     def _():
-        whole_step(coupling_ref, state_ref, low_ref, high_ref, main_ref, send_ref, *scratch[:6], scratch[8])
-        chemistry(rates_ref, pairs_ref, map_ref, coef_ref, q_ref, pre_ref, heat_ref, *scratch[6:8])
+        copies = [pltpu.make_async_copy(inputs[i], scratch[9 + i], sems.at[i]) for i in range(6)]
+        for copy in copies:
+            copy.start()
+        copies[5].wait()
+        whole_step(scratch[14], state_ref, low_ref, high_ref, main_ref, send_ref, *scratch[:6], scratch[8])
+        for copy in copies[:5]:
+            copy.wait()
+        chemistry(*scratch[9:14], pre_ref, heat_ref, *scratch[6:8])
         for y in range(4):
             send_ref[pl.ds(12 + y, PEERS, stride=SLOTS), :] = heat_ref[y]
 
@@ -287,7 +294,6 @@
             gain = jnp.where(lanes >= LANES - HALO, turn(final, LANES - HALO - HALO * plane), gain)
             out_ref[plane, place : place + 8, :] = main_ref[plane, place : place + 8, :] + gain
 
-    send_ref[...] = sent_ref[...]
     winds = 3 * LEVELS
     lanes12 = lane_index(winds)
     zeros = jnp.zeros((LANES - ROWS, LANES), jnp.float32)
@@ -370,6 +376,7 @@
 
 def on_device(state, tracers, coupling, rates, pairs, heat_map, heat_coef):
     planes = state.reshape(PLANES, ROWS, LANES)
+    outside = pl.BlockSpec(memory_space=pltpu.HBM)
     q = tracers.reshape(SPECIES, 128, 128)
 
     count = lax.axis_size("lat")
@@ -383,11 +390,11 @@
     own_far, own_near = pl.pallas_call(
         own_kernel,
         out_shape=(shape(ROWS, LANES),) * 2,
-        in_specs=[VMEM] + [SMEM] * 4 + [VMEM, SMEM],
+        in_specs=[VMEM],
         out_specs=(VMEM,) * 2,
         cost_estimate=cost(1000000, 400000),
         compiler_params=PARAMS,
-    )(planes, *reactants, coupling)
+    )(planes)
     extended = pltpu.VMEM((PLANES, 64, LANES), jnp.float32)
     square = pltpu.VMEM((128, 128), jnp.float32)
 
@@ -400,13 +407,19 @@
                 shape(PLANES, ROWS, LANES),
                 shape(PEERS * SLOTS, LANES),
             ),
-            in_specs=[SMEM] * 4 + [VMEM, SMEM] + [VMEM] * (3 + len(before)),
+            in_specs=[outside] * 6 + [VMEM] * (3 + len(before)),
             out_specs=(VMEM,) * 4,
-            scratch_shapes=[extended] * 6 + [square] * 2 + [pltpu.VMEM((3, 128, 128), jnp.float32)],
+            scratch_shapes=[extended] * 6
+            + [square] * 2
+            + [pltpu.VMEM((3, 128, 128), jnp.float32)]
+            + [pltpu.SMEM(rates.shape, jnp.float32), pltpu.SMEM((3, REACTIONS), jnp.int32)]
+            + [pltpu.SMEM(heat_map.shape, jnp.int32), pltpu.SMEM(heat_coef.shape, jnp.float32)]
+            + [pltpu.VMEM((SPECIES, 128, 128), jnp.float32), pltpu.SMEM(coupling.shape, jnp.float32)]
+            + [pltpu.SemaphoreType.DMA((6,))],
             input_output_aliases={9 + i: i for i in range(len(before))},
             cost_estimate=cost(30000000, 3000000),
             compiler_params=PARAMS,
-        )(*reactants, coupling, planes, low, high, *before)
+        )(*(pltpu.with_memory_space_constraint(x, pltpu.HBM) for x in (*reactants, coupling)), planes, low, high, *before)
 
     done = local(True)
     low, high, once, twice, *done = lax.optimization_barrier((low, high, once, twice, *done))
@@ -437,7 +450,6 @@
     received = lax.all_to_all(
         send.reshape(PEERS, SLOTS, LANES), "lon", split_axis=0, concat_axis=0, tiled=True
     )
-    outside = pl.BlockSpec(memory_space=pltpu.HBM)
     state_out, q_out = pl.pallas_call(
         final_kernel,
         out_shape=(shape(FIELDS, 128, 128), shape(SPECIES, 128, 128)),

time: 60.4 us -> 58.7 us (0.972)
  the two profiles are of different devices: /device:TPU:8 before, /device:TPU:64 now
where the time goes in v5:
time: 58.7 us; the launch traced here: 58.4 us
  starting transfers between devices  24.9 us (42%)
  blocking collectives  17.9 us (30%)
  Pallas kernels  9.75 us (17%)
  waiting for transfers between devices  4.05 us (7%)
  local copies, waits for them, and re-layouts  1.01 us (2%)
  between operations  0.77 us (1%)
    all_to_all x1, blocking collectives, on_device(): lax.all_to_all(send.reshape(PEERS, SLOTS, LANES), 'lon', split_axis=0, co...  17.9 us
    ppermute x1, starting transfers between devices, on_device(): lax.ppermute(planes[:, :BAND], 'lat', [(i + 1, i) for i in range(count -...  14.2 us
    pallas_call x2, Pallas kernels, local(): pl.pallas_call(functools.partial(local_kernel, early), out_shape=(shape(S...  6.23 us
    ppermute x1, starting transfers between devices, on_device(): far_in = lax.ppermute(far, 'grp', [(0, 3), (3, 0), (1, 2), (2, 1)])  4.75 us
    ppermute x1, waiting for transfers between devices, on_device(): lax.ppermute(planes[:, ROWS - BAND:], 'lat', [(i, i + 1) for i in range(c...  4.04 us
    ppermute x1, starting transfers between devices, on_device(): near_in = lax.ppermute(near, 'grp', [(0, 1), (1, 0), (2, 3), (3, 2)])  4.01 us
    ppermute x1, starting transfers between devices, on_device(): lax.ppermute(planes[:, ROWS - BAND:], 'lat', [(i, i + 1) for i in range(c...  1.92 us
    pallas_call x1, Pallas kernels, on_device(): pl.pallas_call(edge_step_kernel, out_shape=(shape(PLANES, ROWS, LANES), s...  1.72 us
  transfers between devices with their start and end apart: 4, of which 1 were waited for; matrix products, arithmetic and copies ran while one was open for 0% of the time, Pallas kernels for 11%

profile of v5, /device:TPU:64, one launch (start us, length us, event | category | flops | bytes accessed | tf_op | source)
XLA Modules:
  0.0 58.4 jit_solution(8989256078125801721)
XLA Ops:
  0.6 0.0 copy-start.1
  0.6 0.0 copy-start.2
  0.7 1.0 %fusion = (f32[20,8,128]{2,1,0:T(8,128)S(1)}, f32[20,8,128]{2,1,0:T(8,128)S(1)}) fusion(f32[20,32,128]{2,1,0:T(8,128)} %bitcast.11), kind=kLoop, calls=%fused_computation.4 | loop fusion | bytes 327680 | tf_op jit(solution)/shard_map/slice | solution.py:384
  1.6 14.2 %collective-permute-start.1 = (f32[20,8,128]{2,1,0:T(8,128)S(1)}, f32[20,8,128]{2,1,0:T(8,128)S(1)}, u32[]{:S(2)}, u32[]{:S(2)}) collective-permute-start(f32[20,8,128]{2,1,0:T(8,128)S(1)} %get-tuple-element.64), channel_id=1, source_target_pairs={{32,0},{64,32},{96,64},{128,96},{160,128},{192,160},{224,192},{33,... | collective-permute-start | bytes 245768 | tf_op jit(solution)/shard_map/ppermute | solution.py:384
  15.8 1.9 %collective-permute-start = (f32[20,8,128]{2,1,0:T(8,128)S(1)}, f32[20,8,128]{2,1,0:T(8,128)S(1)}, u32[]{:S(2)}, u32[]{:S(2)}) collective-permute-start(f32[20,8,128]{2,1,0:T(8,128)S(1)} %get-tuple-element.65), channel_id=1, source_target_pairs={{0,32},{32,64},{64,96},{96,128},{128,160},{160,192},{192,224},{1,3... | collective-permute-start | bytes 245768 | tf_op jit(solution)/shard_map/ppermute | solution.py:383
  17.8 0.0 copy-done.2
  17.8 0.1 multiply_reduce_fusion
  17.9 0.0 copy-done.1
  17.9 0.2 shard_map.87
  18.1 0.0 collective-permute-done.1.refs_8_.high_ref
  18.1 4.0 %collective-permute-done.refs_7_.low_ref = f32[20,8,128]{2,1,0:T(8,128)S(1)} collective-permute-done((f32[20,8,128]{2,1,0:T(8,128)S(1)}, f32[20,8,128]{2,1,0:T(8,128)S(1)}, u32[]{:S(2)}, u32[]{:S(2)}) %collective-permute-start) | collective-permute-done | bytes 81952 | tf_op jit(solution)/shard_map/ppermute | solution.py:383
  22.2 0.1 shard_map.86
  22.2 0.1 shard_map.88
  22.4 4.7 %collective-permute-start.2 = (f32[48,128]{1,0:T(8,128)S(1)}, f32[48,128]{1,0:T(8,128)S(1)}, u32[]{:S(2)}, u32[]{:S(2)}) collective-permute-start(f32[48,128]{1,0:T(8,128)S(1)} %get-tuple-element.57), channel_id=1, source_target_pairs={{0,768},{768,0},{256,512},{512,256},{1,769},{769,1},{257,513},{513... | collective-permute-start | bytes 73736 | tf_op jit(solution)/shard_map/ppermute | solution.py:435
  27.1 4.0 %collective-permute-start.3 = (f32[48,128]{1,0:T(8,128)S(1)}, f32[48,128]{1,0:T(8,128)S(1)}, u32[]{:S(2)}, u32[]{:S(2)}) collective-permute-start(f32[48,128]{1,0:T(8,128)S(1)} %get-tuple-element.58), channel_id=1, source_target_pairs={{0,256},{256,0},{512,768},{768,512},{1,257},{257,1},{513,769},{769... | collective-permute-start | bytes 73736 | tf_op jit(solution)/shard_map/ppermute | solution.py:436
  31.2 6.2 %shard_map.89 = (f32[12,128,128]{2,1,0:T(8,128)S(1)}, f32[4,32,128]{2,1,0:T(8,128)S(1)}, f32[20,32,128]{2,1,0:T(8,128)S(1)}, f32[512,128]{1,0:T(8,128)S(1)}) custom-call(f32[24]{0:T(128)} %refs_0_.3, s32[3,24]{1,0:T(4,128)} %bitcast.19, s32[12]{0:T(128)} %refs_2_.3, ...), custom_call_target="tpu_custom_call", output_to_operand_aliasing={{0}: (9, {}), {1}: (10, {}), {2}: (11, {}), {3}: (12, {})} | custom-call | flops 30000000 | bytes 3000000 | tf_op jit(solution)/shard_map/pallas_call | solution.py:402
  37.3 0.0 copy-start
  37.4 0.0 collective-permute-done.2.far_ref
  37.4 0.0 collective-permute-done.3.near_ref
  37.4 1.7 %shard_map.90 = (f32[20,32,128]{2,1,0:T(8,128)S(1)}, f32[512,128]{1,0:T(8,128)S(1)}) custom-call(f32[5,5]{1,0:T(8,128)S(1)} %get-tuple-element.37.once_ref, f32[5,5]{1,0:T(8,128)S(1)} %get-tuple-element.38.twice_ref, f32[20,32,128]{2,1,0:T(8,128)S(1)} %get-tuple-element.55.main_ref, ...), custom_call_target="tpu_custom_call", output_to_operand_aliasing={{1}: (3, {})} | custom-call | flops 2000000 | bytes 1000000 | tf_op jit(solution)/shard_map/pallas_call | solution.py:439
  39.1 17.9 %all_to_all.5 = f32[32,16,128]{2,1,0:T(8,128)S(1)} all-to-all(f32[32,16,128]{2,1,0:T(8,128)S(1)} %bitcast.15), channel_id=1, replica_groups=mesh['grp'=4,'lat'=8,'lon'=32] {'lon'}, dimensions={0} | all-to-all | bytes 524288 | tf_op jit(solution)/shard_map/all_to_all | solution.py:450
  57.0 0.0 copy-done
  57.0 1.4 %shard_map.91 = (f32[5,128,128]{2,1,0:T(8,128)}, f32[12,128,128]{2,1,0:T(8,128)}) custom-call(f32[512,128]{1,0:T(8,128)S(1)} %bitcast.16, f32[5,128,128]{2,1,0:T(8,128)S(1)} %bitcast.17, f32[12,128,128]{2,1,0:T(8,128)S(1)} %bitcast.10, f32[12,128,128]{2,1,0:T(8,128)S(1)} %get-tuple-element.61.pre_ref), custom_call_target="tpu_custom_call" | custom-call | flops 10000000 | bytes 2500000 | tf_op jit(solution)/shard_map/pallas_call | solution.py:453
  (1 shorter events, 0.0 us)
Async XLA Ops:
  0.6 17.3 %copy-start.1 = (f32[5,4,32,128]{3,2,1,0:T(8,128)S(1)}, f32[5,4,32,128]{3,2,1,0:T(8,128)}, u32[]{:S(2)}) copy-start(f32[5,4,32,128]{3,2,1,0:T(8,128)} %param.7) | copy-start | bytes 983044
  0.6 17.1 %copy-start.2 = (f32[5,5]{1,0:T(8,128)S(1)}, f32[5,5]{1,0:T(8,128)}, u32[]{:S(2)}) copy-start(f32[5,5]{1,0:T(8,128)} %refs_5_.3) | copy-start | bytes 304
  1.6 16.5 %collective-permute-start.1 = (f32[20,8,128]{2,1,0:T(8,128)S(1)}, f32[20,8,128]{2,1,0:T(8,128)S(1)}, u32[]{:S(2)}, u32[]{:S(2)}) collective-permute-start(f32[20,8,128]{2,1,0:T(8,128)S(1)} %get-tuple-element.64), channel_id=1, source_target_pairs={{32,0},{64,32},{96,64},{128,96},{160,128},{192,160},{224,192},{33,... | collective-permute-start | bytes 245768 | tf_op jit(solution)/shard_map/ppermute | solution.py:384
  15.8 6.3 %collective-permute-start = (f32[20,8,128]{2,1,0:T(8,128)S(1)}, f32[20,8,128]{2,1,0:T(8,128)S(1)}, u32[]{:S(2)}, u32[]{:S(2)}) collective-permute-start(f32[20,8,128]{2,1,0:T(8,128)S(1)} %get-tuple-element.65), channel_id=1, source_target_pairs={{0,32},{32,64},{64,96},{96,128},{128,160},{160,192},{192,224},{1,3... | collective-permute-start | bytes 245768 | tf_op jit(solution)/shard_map/ppermute | solution.py:383
  22.4 15.0 %collective-permute-start.2 = (f32[48,128]{1,0:T(8,128)S(1)}, f32[48,128]{1,0:T(8,128)S(1)}, u32[]{:S(2)}, u32[]{:S(2)}) collective-permute-start(f32[48,128]{1,0:T(8,128)S(1)} %get-tuple-element.57), channel_id=1, source_target_pairs={{0,768},{768,0},{256,512},{512,256},{1,769},{769,1},{257,513},{513... | collective-permute-start | bytes 73736 | tf_op jit(solution)/shard_map/ppermute | solution.py:435
  27.1 10.2 %collective-permute-start.3 = (f32[48,128]{1,0:T(8,128)S(1)}, f32[48,128]{1,0:T(8,128)S(1)}, u32[]{:S(2)}, u32[]{:S(2)}) collective-permute-start(f32[48,128]{1,0:T(8,128)S(1)} %get-tuple-element.58), channel_id=1, source_target_pairs={{0,256},{256,0},{512,768},{768,512},{1,257},{257,1},{513,769},{769... | collective-permute-start | bytes 73736 | tf_op jit(solution)/shard_map/ppermute | solution.py:436
  37.3 19.7 %copy-start = (f32[12,32,4,128]{3,2,1,0:T(4,128)S(1)}, f32[12,32,4,128]{3,2,1,0:T(4,128)}, u32[]{:S(2)}) copy-start(f32[12,32,4,128]{3,2,1,0:T(4,128)} %param.8) | copy-start | bytes 2359300

commit v6 on v5

--- a/solution.py
+++ b/solution.py
@@ -6,6 +6,7 @@
 from jax.experimental import pallas as pl
 from jax.experimental.pallas import tpu as pltpu
 from jax.sharding import PartitionSpec as P
+
 
 FIELDS = 5
 LEVELS = 4
@@ -25,27 +26,31 @@
     return lax.broadcasted_iota(jnp.int32, (rows, LANES), 1)
 
 
-def packed(source):
-    lanes = lane_index(source.shape[1])
-    left = source[0]
-    right = pltpu.roll(source[0], HALO, 1)
+def packed(tiles):
+    lanes = lane_index(tiles[0].shape[0])
+    left = tiles[0]
+    right = pltpu.roll(tiles[0], HALO, 1)
     for plane in range(1, PLANES):
         keep = lanes >= HALO * plane
-        left = jnp.where(keep, pltpu.roll(source[plane], HALO * plane, 1), left)
-        right = jnp.where(keep, pltpu.roll(source[plane], HALO * plane + HALO, 1), right)
+        left = jnp.where(keep, pltpu.roll(tiles[plane], HALO * plane, 1), left)
+        right = jnp.where(keep, pltpu.roll(tiles[plane], (HALO * plane + HALO) % LANES, 1), right)
     odd = lax.rem(lax.axis_index("grp"), 2) == 1
     return jnp.where(odd, right, left), jnp.where(odd, left, right)
 
 
 def own_kernel(state_ref, far_ref, near_ref):
-    far_ref[...], near_ref[...] = packed(state_ref)
+    far_ref[...], near_ref[...] = packed([state_ref[plane] for plane in range(PLANES)])
 
 
 def pack_kernel(low_ref, high_ref, own_far_ref, own_near_ref, far_ref, near_ref):
     far_ref[BAND : BAND + ROWS] = own_far_ref[...]
     near_ref[BAND : BAND + ROWS] = own_near_ref[...]
-    far_ref[:BAND], near_ref[:BAND] = packed(low_ref)
-    far_ref[BAND + ROWS :], near_ref[BAND + ROWS :] = packed(high_ref)
+    unused = jnp.zeros((BAND - HALO, LANES), jnp.float32)
+    low = [low_ref[HALO * plane : HALO * plane + HALO] for plane in range(PLANES)]
+    high = [high_ref[HALO * plane : HALO * plane + HALO] for plane in range(PLANES)]
+    for ref, under, over in zip((far_ref, near_ref), packed(low), packed(high), strict=True):
+        ref[:BAND] = jnp.concatenate([unused, under], 0)
+        ref[BAND + ROWS :] = jnp.concatenate([over, unused], 0)
 
 
 def regroup(chunks):
@@ -123,9 +128,9 @@
 
     sb[...] = jnp.zeros_like(sb)
     for plane in range(PLANES):
-        sa[plane, base - BAND : base, :] = low_ref[plane]
+        sa[plane, base - HALO : base, :] = low_ref[HALO * plane : HALO * plane + HALO]
         sa[plane, base : base + ROWS, :] = state_ref[plane]
-        sa[plane, base + ROWS : base + ROWS + BAND, :] = high_ref[plane]
+        sa[plane, base + ROWS : base + ROWS + HALO, :] = high_ref[HALO * plane : HALO * plane + HALO]
 
     lane8 = lane_index(8)
     weights = [
@@ -380,8 +385,8 @@
     q = tracers.reshape(SPECIES, 128, 128)
 
     count = lax.axis_size("lat")
-    low = lax.ppermute(planes[:, ROWS - BAND :], "lat", [(i, i + 1) for i in range(count - 1)])
-    high = lax.ppermute(planes[:, :BAND], "lat", [(i + 1, i) for i in range(count - 1)])
+    high = lax.ppermute(planes[:, :HALO].reshape(PLANES * HALO, LANES), "lat", [(i + 1, i) for i in range(count - 1)])
+    low = lax.ppermute(planes[:, ROWS - HALO :].reshape(PLANES * HALO, LANES), "lat", [(i, i + 1) for i in range(count - 1)])
     once = jnp.eye(FIELDS, dtype=jnp.float32) + coupling
     squared = jnp.sum(coupling[:, :, None] * coupling[None, :, :], 1)
     twice = once + 0.5 * squared
@@ -479,6 +484,4 @@
         P(),
     )
     out_specs = (P(None, "lon", "lat", "grp"), P(None, "lat", ("grp", "lon"), None))
-    return jax.shard_map(
-        on_device, mesh=mesh, in_specs=in_specs, out_specs=out_specs, check_vma=False
-    )
+    return jax.shard_map(on_device, mesh=mesh, in_specs=in_specs, out_specs=out_specs, check_vma=False)

time: 58.7 us -> 59.7 us (1.017)
  the two profiles are of different devices: /device:TPU:64 before, /device:TPU:8 now
where the time goes in v6:
time: 59.7 us; the launch traced here: 59.4 us
  blocking collectives  22.6 us (38%)
  starting transfers between devices  19.6 us (33%)
  Pallas kernels  9.75 us (16%)
  waiting for transfers between devices  5.54 us (9%)
  local copies, waits for them, and re-layouts  1.02 us (2%)
  between operations  0.77 us (1%)
    all_to_all x1, blocking collectives, on_device(): lax.all_to_all(send.reshape(PEERS, SLOTS, LANES), 'lon', split_axis=0, co...  22.6 us
    ppermute x1, starting transfers between devices, on_device(): far_in = lax.ppermute(far, 'grp', [(0, 3), (3, 0), (1, 2), (2, 1)])  10 us
    pallas_call x2, Pallas kernels, local(): pl.pallas_call(functools.partial(local_kernel, early), out_shape=(shape(S...  6.23 us
    ppermute x1, waiting for transfers between devices, on_device(): lax.ppermute(planes[:, :HALO].reshape(PLANES * HALO, LANES), 'lat', [(i +...  4.66 us
    ppermute x1, starting transfers between devices, on_device(): lax.ppermute(planes[:, ROWS - HALO:].reshape(PLANES * HALO, LANES), 'lat'...  4.28 us
    ppermute x1, starting transfers between devices, on_device(): near_in = lax.ppermute(near, 'grp', [(0, 1), (1, 0), (2, 3), (3, 2)])  4.01 us
    pallas_call x1, Pallas kernels, on_device(): pl.pallas_call(edge_step_kernel, out_shape=(shape(PLANES, ROWS, LANES), s...  1.72 us
    pallas_call x1, Pallas kernels, on_device(): pl.pallas_call(final_kernel, out_shape=(shape(FIELDS, 128, 128), shape(SP...  1.43 us
  transfers between devices with their start and end apart: 4, of which 3 were waited for; matrix products, arithmetic and copies ran while one was open for 0% of the time, Pallas kernels for 1%

profile of v6, /device:TPU:8, one launch (start us, length us, event | category | flops | bytes accessed | tf_op | source)
XLA Modules:
  0.0 59.4 jit_solution(17664070219425123100)
XLA Ops:
  0.6 0.0 copy-start.1
  0.6 1.0 %fusion = (f32[20,6,128]{2,1,0:T(8,128)S(1)}, f32[20,6,128]{2,1,0:T(8,128)S(1)}) fusion(f32[20,32,128]{2,1,0:T(8,128)} %bitcast.11), kind=kLoop, calls=%fused_computation.4 | loop fusion | bytes 245760 | tf_op jit(solution)/shard_map/slice | solution.py:388
  1.6 4.3 %collective-permute-start = (f32[120,128]{1,0:T(8,128)S(1)}, f32[120,128]{1,0:T(8,128)S(1)}, u32[]{:S(2)}, u32[]{:S(2)}) collective-permute-start(f32[120,128]{1,0:T(8,128)S(1)} %reshape.34), channel_id=1, source_target_pairs={{0,32},{32,64},{64,96},{96,128},{128,160},{160,192},{192,224},{1,3... | collective-permute-start | bytes 184328 | tf_op jit(solution)/shard_map/ppermute | solution.py:389
  5.9 0.0 copy-start.2
  6.0 1.3 %collective-permute-start.1 = (f32[120,128]{1,0:T(8,128)S(1)}, f32[120,128]{1,0:T(8,128)S(1)}, u32[]{:S(2)}, u32[]{:S(2)}) collective-permute-start(f32[120,128]{1,0:T(8,128)S(1)} %reshape.35), channel_id=1, source_target_pairs={{32,0},{64,32},{96,64},{128,96},{160,128},{192,160},{224,192},{33,... | collective-permute-start | bytes 184328 | tf_op jit(solution)/shard_map/ppermute | solution.py:388
  7.3 0.0 copy-done.2
  7.3 0.1 multiply_reduce_fusion
  7.4 0.0 copy-done.1
  7.4 0.2 shard_map.87
  7.6 0.2 collective-permute-done.refs_7_.low_ref
  7.8 4.7 %collective-permute-done.1.refs_8_.high_ref = f32[120,128]{1,0:T(8,128)S(1)} collective-permute-done((f32[120,128]{1,0:T(8,128)S(1)}, f32[120,128]{1,0:T(8,128)S(1)}, u32[]{:S(2)}, u32[]{:S(2)}) %collective-permute-start.1) | collective-permute-done | bytes 61472 | tf_op jit(solution)/shard_map/ppermute | solution.py:388
  12.4 6.2 %shard_map.86 = (f32[12,128,128]{2,1,0:T(8,128)S(1)}, f32[4,32,128]{2,1,0:T(8,128)S(1)}, f32[20,32,128]{2,1,0:T(8,128)S(1)}, f32[512,128]{1,0:T(8,128)S(1)}) custom-call(f32[24]{0:T(128)} %refs_0_.3, s32[3,24]{1,0:T(4,128)} %bitcast.18, s32[12]{0:T(128)} %refs_2_.3, f32[4]{0:T(128)} %refs_3_.3, f32[12,128,128]{2,1,0:T(8,128)} %bitcast.8, f32[5,5]{1,0:T(8,128)} %refs_5_.3, ...), custom_call_target="tpu_custom_call" | custom-call | flops 30000000 | bytes 3000000 | tf_op jit(solution)/shard_map/pallas_call | solution.py:407
  18.6 0.1 shard_map.88
  18.8 10.0 %collective-permute-start.2 = (f32[48,128]{1,0:T(8,128)S(1)}, f32[48,128]{1,0:T(8,128)S(1)}, u32[]{:S(2)}, u32[]{:S(2)}) collective-permute-start(f32[48,128]{1,0:T(8,128)S(1)} %get-tuple-element.57), channel_id=1, source_target_pairs={{0,768},{768,0},{256,512},{512,256},{1,769},{769,1},{257,513},{513... | collective-permute-start | bytes 73736 | tf_op jit(solution)/shard_map/ppermute | solution.py:440
  28.8 4.0 %collective-permute-start.3 = (f32[48,128]{1,0:T(8,128)S(1)}, f32[48,128]{1,0:T(8,128)S(1)}, u32[]{:S(2)}, u32[]{:S(2)}) collective-permute-start(f32[48,128]{1,0:T(8,128)S(1)} %get-tuple-element.58), channel_id=1, source_target_pairs={{0,256},{256,0},{512,768},{768,512},{1,257},{257,1},{513,769},{769... | collective-permute-start | bytes 73736 | tf_op jit(solution)/shard_map/ppermute | solution.py:441
  32.8 0.1 shard_map.89
  32.9 0.0 copy-start
  32.9 0.0 collective-permute-done.2.far_ref
  32.9 0.7 %collective-permute-done.3.near_ref = f32[48,128]{1,0:T(8,128)S(1)} collective-permute-done((f32[48,128]{1,0:T(8,128)S(1)}, f32[48,128]{1,0:T(8,128)S(1)}, u32[]{:S(2)}, u32[]{:S(2)}) %collective-permute-start.3) | collective-permute-done | bytes 24608 | tf_op jit(solution)/shard_map/ppermute | solution.py:441
  33.6 1.7 %shard_map.90 = (f32[20,32,128]{2,1,0:T(8,128)S(1)}, f32[512,128]{1,0:T(8,128)S(1)}) custom-call(f32[5,5]{1,0:T(8,128)S(1)} %get-tuple-element.37.once_ref, f32[5,5]{1,0:T(8,128)S(1)} %get-tuple-element.38.twice_ref, f32[20,32,128]{2,1,0:T(8,128)S(1)} %get-tuple-element.55.main_ref, ...), custom_call_target="tpu_custom_call", output_to_operand_aliasing={{1}: (3, {})} | custom-call | flops 2000000 | bytes 1000000 | tf_op jit(solution)/shard_map/pallas_call | solution.py:444
  35.3 22.6 %all_to_all.5 = f32[32,16,128]{2,1,0:T(8,128)S(1)} all-to-all(f32[32,16,128]{2,1,0:T(8,128)S(1)} %bitcast.15), channel_id=1, replica_groups=mesh['grp'=4,'lat'=8,'lon'=32] {'lon'}, dimensions={0} | all-to-all | bytes 524288 | tf_op jit(solution)/shard_map/all_to_all | solution.py:455
  58.0 0.0 copy-done
  58.0 1.4 %shard_map.91 = (f32[5,128,128]{2,1,0:T(8,128)}, f32[12,128,128]{2,1,0:T(8,128)}) custom-call(f32[512,128]{1,0:T(8,128)S(1)} %bitcast.16, f32[5,128,128]{2,1,0:T(8,128)S(1)} %bitcast.17, f32[12,128,128]{2,1,0:T(8,128)S(1)} %bitcast.10, f32[12,128,128]{2,1,0:T(8,128)S(1)} %get-tuple-element.61.pre_ref), custom_call_target="tpu_custom_call" | custom-call | flops 10000000 | bytes 2500000 | tf_op jit(solution)/shard_map/pallas_call | solution.py:458
  (3 shorter events, 0.0 us)
Async XLA Ops:
  0.6 6.7 %copy-start.1 = (f32[5,4,32,128]{3,2,1,0:T(8,128)S(1)}, f32[5,4,32,128]{3,2,1,0:T(8,128)}, u32[]{:S(2)}) copy-start(f32[5,4,32,128]{3,2,1,0:T(8,128)} %param.7) | copy-start | bytes 983044
  1.6 6.1 %collective-permute-start = (f32[120,128]{1,0:T(8,128)S(1)}, f32[120,128]{1,0:T(8,128)S(1)}, u32[]{:S(2)}, u32[]{:S(2)}) collective-permute-start(f32[120,128]{1,0:T(8,128)S(1)} %reshape.34), channel_id=1, source_target_pairs={{0,32},{32,64},{64,96},{96,128},{128,160},{160,192},{192,224},{1,3... | collective-permute-start | bytes 184328 | tf_op jit(solution)/shard_map/ppermute | solution.py:389
  5.9 1.3 %copy-start.2 = (f32[5,5]{1,0:T(8,128)S(1)}, f32[5,5]{1,0:T(8,128)}, u32[]{:S(2)}) copy-start(f32[5,5]{1,0:T(8,128)} %refs_5_.3) | copy-start | bytes 304
  6.0 6.5 %collective-permute-start.1 = (f32[120,128]{1,0:T(8,128)S(1)}, f32[120,128]{1,0:T(8,128)S(1)}, u32[]{:S(2)}, u32[]{:S(2)}) collective-permute-start(f32[120,128]{1,0:T(8,128)S(1)} %reshape.35), channel_id=1, source_target_pairs={{32,0},{64,32},{96,64},{128,96},{160,128},{192,160},{224,192},{33,... | collective-permute-start | bytes 184328 | tf_op jit(solution)/shard_map/ppermute | solution.py:388
  18.8 14.1 %collective-permute-start.2 = (f32[48,128]{1,0:T(8,128)S(1)}, f32[48,128]{1,0:T(8,128)S(1)}, u32[]{:S(2)}, u32[]{:S(2)}) collective-permute-start(f32[48,128]{1,0:T(8,128)S(1)} %get-tuple-element.57), channel_id=1, source_target_pairs={{0,768},{768,0},{256,512},{512,256},{1,769},{769,1},{257,513},{513... | collective-permute-start | bytes 73736 | tf_op jit(solution)/shard_map/ppermute | solution.py:440
  28.8 4.8 %collective-permute-start.3 = (f32[48,128]{1,0:T(8,128)S(1)}, f32[48,128]{1,0:T(8,128)S(1)}, u32[]{:S(2)}, u32[]{:S(2)}) collective-permute-start(f32[48,128]{1,0:T(8,128)S(1)} %get-tuple-element.58), channel_id=1, source_target_pairs={{0,256},{256,0},{512,768},{768,512},{1,257},{257,1},{513,769},{769... | collective-permute-start | bytes 73736 | tf_op jit(solution)/shard_map/ppermute | solution.py:441
  32.9 25.1 %copy-start = (f32[12,32,4,128]{3,2,1,0:T(4,128)S(1)}, f32[12,32,4,128]{3,2,1,0:T(4,128)}, u32[]{:S(2)}) copy-start(f32[12,32,4,128]{3,2,1,0:T(4,128)} %param.8) | copy-start | bytes 2359300
